TPU v7x, 512 devices: a whole 4x4x16 slice. The times are simulated.
512 devices in a mesh: grid: 64 (over y, z), state: 8 (over x, core).
Axes of the slice: x: 4, y: 4, z: 16, core: 2. Of those that a mesh axis runs over, the one named last changes fastest.
Arguments:
- orbitals: float32 [8, 512, 64, 128], P('state', 'grid'), may hold values from -6 to 6
- potential: float32 [512, 64, 128], P('grid'), may hold values from 0 to 2
Outputs:
- corrections: float32 [8, 512, 64, 128], P('state', 'grid')
- correlation_gram: float32 [8, 8], P('state')
All inputs are finite; a program needn't handle non-finite values.
Results may differ from a plain program's by a relative error of at most 0.00095.
Values may be sent and summed in bfloat16 or wider, within the bound.
A program may use at most 64 MiB of HBM per device.

v0:
```python
import jax
import jax.numpy as jnp
from jax import lax
from jax.sharding import PartitionSpec as P

LEVELS = 4
COARSE_SWEEPS = 3


CENTER = -2.5
NEAR_COEF = 4.0 / 3.0
FAR_COEF = -1.0 / 12.0
SHIFT_TERM = 0.25
DAMPING = 2.0 / 3.0


def with_halo(block, sides, width):
    for axis, dim in sides:
        count = lax.axis_size(axis)
        forward = [(i, i + 1) for i in range(count - 1)]
        forward.append((count - 1, 0))
        backward = [(target, source) for source, target in forward]
        low = lax.ppermute(
            lax.slice_in_dim(block, block.shape[dim] - width, None, axis=dim), axis, forward
        )
        high = lax.ppermute(lax.slice_in_dim(block, 0, width, axis=dim), axis, backward)
        block = jnp.concatenate([low, block, high], axis=dim)
    return block


def laplace_four(values, axis):
    near = jnp.roll(values, 1, axis) + jnp.roll(values, -1, axis)
    far = jnp.roll(values, 2, axis) + jnp.roll(values, -2, axis)
    return CENTER * values + NEAR_COEF * near + FAR_COEF * far


def face_halo(values):
    return with_halo(values.astype(jnp.bfloat16), (("grid", 1),), 1).astype(values.dtype)


def level_apply(values, padded, inverse):
    beside = padded[:, 2:] + padded[:, :-2]
    beside = beside + jnp.roll(values, 1, 2) + jnp.roll(values, -1, 2)
    beside = beside + jnp.roll(values, 1, 3) + jnp.roll(values, -1, 3)
    return (SHIFT_TERM + 3.0 * inverse) * values - 0.5 * inverse * beside


def restrict(values):
    count, sx, sy, sz = values.shape
    shaped = values.reshape(count, sx // 2, 2, sy // 2, 2, sz // 2, 2)
    return jnp.mean(shaped, axis=(2, 4, 6))


def prolong(values):
    return jnp.repeat(jnp.repeat(jnp.repeat(values, 2, 1), 2, 2), 2, 3)


def jacobi_sweep(iterate, source, inverse, padder):
    diagonal = SHIFT_TERM + 3.0 * inverse
    applied = level_apply(iterate, padder(iterate), inverse)
    return iterate + DAMPING * (source - applied) / diagonal


def coarse_solve(source, inverse, padder):
    diagonal = SHIFT_TERM + 3.0 * inverse
    iterate = DAMPING * source / diagonal
    for repeat in range(COARSE_SWEEPS - 1):
        iterate = jacobi_sweep(iterate, source, inverse, padder)
    return iterate


def vcycle(source, depth_level):
    inverse = 0.25**depth_level
    diagonal = SHIFT_TERM + 3.0 * inverse
    if depth_level == LEVELS - 1:
        return coarse_solve(source, inverse, face_halo)
    iterate = DAMPING * source / diagonal
    remainder = source - level_apply(iterate, face_halo(iterate), inverse)
    coarse_error = vcycle(restrict(remainder), depth_level + 1)
    iterate = iterate + prolong(coarse_error)
    return jacobi_sweep(iterate, source, inverse, face_halo)


def on_device(orbitals, potential):
    padded = with_halo(orbitals, (("grid", 1),), 2)
    near = padded[:, 3:-1] + padded[:, 1:-3]
    far = padded[:, 4:] + padded[:, :-4]
    lap_first = CENTER * orbitals + NEAR_COEF * near + FAR_COEF * far
    lap = lap_first + laplace_four(orbitals, 2) + laplace_four(orbitals, 3)
    hpsi = -0.5 * lap + potential[None] * orbitals
    numer, denom = lax.psum(
        (jnp.sum(orbitals * hpsi, axis=(1, 2, 3)), jnp.sum(orbitals * orbitals, axis=(1, 2, 3))),
        "grid",
    )
    energy = numer / denom
    residual = hpsi - energy[:, None, None, None] * orbitals
    corrections = vcycle(residual, 0)
    count = corrections.shape[0]
    rounded = corrections.astype(jnp.bfloat16).reshape(count, -1)
    row_block = jnp.einsum(
        "ac,bc->ab",
        rounded,
        lax.all_gather(rounded, "state", axis=0, tiled=True),
        preferred_element_type=jnp.float32,
    )
    summed = lax.psum(row_block, "grid")
    correlation_gram = summed / jnp.float32(rounded.shape[1] * lax.axis_size("grid"))
    return (corrections, correlation_gram)


def solution(mesh):
    placed = (P("state", "grid", None, None), P("grid", None, None))
    return jax.shard_map(
        on_device,
        mesh=mesh,
        in_specs=placed,
        out_specs=(P("state", "grid", None, None), P("state", None)),
        check_vma=False,
    )
```

profile of v0, /device:TPU:2, one launch (start us, length us, event | category | flops | bytes accessed | tf_op | source)
XLA Modules:
  0.0 495.3 jit_solution(615986933523737960)
XLA Ops:
  7.2 1.5 fusion.122
  8.7 3.8 collective-permute-start.1
  12.5 11.9 %collective-permute-start = (f32[1,2,64,128]{3,2,1,0:T(8,128)}, f32[1,2,64,128]{3,2,1,0:T(8,128)S(1)}, u32[]{:S(2)}, u32[]{:S(2)}) collective-permute-start(f32[1,2,64,128]{3,2,1,0:T(8,128)} %get-tuple-element.64), channel_id=1, source_target_pairs={{8,0},{16,8},{24,16},{32,24},{40,32},{48,40},{56,48},{64,56},{72,6... | collective-permute-start | bytes 196616 | tf_op jit(solution)/shard_map/ppermute | solution.py:26
  36.9 2.0 copy.153
  40.9 4.4 multiply_reduce_fusion
  45.3 140.7 %all-reduce = (f32[1]{0:T(128)}, f32[1]{0:T(128)}) all-reduce(f32[1]{0:T(128)} %bitcast.1, f32[1]{0:T(128)} %bitcast.2), channel_id=1, replica_groups=mesh['grid'=64,'state'=8] {'grid'}, use_global_device_ids=true, to_apply=%region_1.2 | all-reduce | flops 2 | bytes 16 | tf_op jit(solution)/shard_map/psum | solution.py:91
  188.0 1.9 collective-permute-start.2
  190.0 7.2 %collective-permute-start.3 = (bf16[1,1,64,128]{2,1,3,0:T(2,128)(2,1)S(1)}, bf16[1,1,64,128]{2,1,3,0:T(2,128)(2,1)S(1)}, u32[]{:S(2)}, u32[]{:S(2)}) collective-permute-start(bf16[1,1,64,128]{2,1,3,0:T(2,128)(2,1)S(1)} %get-tuple-element.59), channel_id=1, source_target_pairs={{8,0},{16,8},{24,16},{32,24},{40,32},{48,40},{56,48},{64,56},{72,6... | collective-permute-start | bytes 49160 | tf_op jit(solution)/shard_map/ppermute | solution.py:26
  197.5 1.6 collective-permute-done.3
  200.1 18.1 %reshape.809 = f32[4,2,32,2,64,2]{5,4,3,2,1,0:T(8,128)} reshape(f32[1,8,64,128]{3,2,1,0:T(8,128)S(1)} %copy.140) | data formatting | bytes 524288 | tf_op jit(solution)/shard_map/reshape | solution.py:50
  218.2 7.0 %reduce_sum.60 = f32[4,32,64]{2,1,0:T(8,128)S(1)} reduce(f32[4,2,32,2,64,2]{5,4,3,2,1,0:T(8,128)} %reshape.809, f32[]{:T(128)} %constant.51.clone.1), dimensions={1,3,5}, to_apply=%region_4.5 | reduce | flops 57344 | bytes 294916 | tf_op jit(solution)/shard_map/reduce_sum | solution.py:51
  225.4 1.9 collective-permute-start.4
  227.3 7.6 %collective-permute-start.5 = (bf16[1,1,32,64]{3,2,1,0:T(8,128)(2,1)S(1)}, bf16[1,1,32,64]{3,2,1,0:T(8,128)(2,1)S(1)}, u32[]{:S(2)}, u32[]{:S(2)}) collective-permute-start(bf16[1,1,32,64]{3,2,1,0:T(8,128)(2,1)S(1)} %get-tuple-element.91), channel_id=1, source_target_pairs={{8,0},{16,8},{24,16},{32,24},{40,32},{48,40},{56,48},{64,56},{72,6... | collective-permute-start | bytes 12296 | tf_op jit(solution)/shard_map/ppermute | solution.py:26
  236.4 2.1 reshape.810
  239.0 1.9 collective-permute-start.6
  240.9 7.5 %collective-permute-start.7 = (bf16[1,1,16,32]{3,2,1,0:T(8,128)(2,1)S(1)}, bf16[1,1,16,32]{3,2,1,0:T(8,128)(2,1)S(1)}, u32[]{:S(2)}, u32[]{:S(2)}) collective-permute-start(bf16[1,1,16,32]{3,2,1,0:T(8,128)(2,1)S(1)} %get-tuple-element.116), channel_id=1, source_target_pairs={{8,0},{16,8},{24,16},{32,24},{40,32},{48,40},{56,48},{64,56},{72,6... | collective-permute-start | bytes 3080 | tf_op jit(solution)/shard_map/ppermute | solution.py:26
  250.2 7.5 %collective-permute-start.9 = (bf16[1,1,8,16]{3,2,1,0:T(8,128)(2,1)S(1)}, bf16[1,1,8,16]{3,2,1,0:T(8,128)(2,1)S(1)}, u32[]{:S(2)}, u32[]{:S(2)}) collective-permute-start(bf16[1,1,8,16]{3,2,1,0:T(8,128)(2,1)S(1)} %get-tuple-element.126), channel_id=1, source_target_pairs={{8,0},{16,8},{24,16},{32,24},{40,32},{48,40},{56,48},{64,56},{72,6... | collective-permute-start | bytes 776 | tf_op jit(solution)/shard_map/ppermute | solution.py:26
  257.7 1.9 collective-permute-start.8
  259.7 6.8 %collective-permute-done.8 = bf16[1,1,8,16]{3,2,1,0:T(8,128)(2,1)S(1)} collective-permute-done((bf16[1,1,8,16]{3,2,1,0:T(8,128)(2,1)S(1)}, bf16[1,1,8,16]{3,2,1,0:T(8,128)(2,1)S(1)}, u32[]{:S(2)}, u32[]{:S(2)}) %collective-permute-start.8) | collective-permute-done | bytes 288 | tf_op jit(solution)/shard_map/ppermute | solution.py:23
  266.7 1.9 collective-permute-start.11
  268.7 3.9 collective-permute-start.10
  272.6 4.8 collective-permute-done.10
  277.9 1.9 collective-permute-start.12
  279.8 7.2 %collective-permute-start.13 = (bf16[1,1,16,32]{3,2,1,0:T(8,128)(2,1)S(1)}, bf16[1,1,16,32]{3,2,1,0:T(8,128)(2,1)S(1)}, u32[]{:S(2)}, u32[]{:S(2)}) collective-permute-start(bf16[1,1,16,32]{3,2,1,0:T(8,128)(2,1)S(1)} %get-tuple-element.114), channel_id=1, source_target_pairs={{8,0},{16,8},{24,16},{32,24},{40,32},{48,40},{56,48},{64,56},{72,6... | collective-permute-start | bytes 3080 | tf_op jit(solution)/shard_map/ppermute | solution.py:26
  289.0 1.9 collective-permute-start.14
  290.9 7.5 %collective-permute-start.15 = (bf16[1,1,32,64]{3,2,1,0:T(8,128)(2,1)S(1)}, bf16[1,1,32,64]{3,2,1,0:T(8,128)(2,1)S(1)}, u32[]{:S(2)}, u32[]{:S(2)}) collective-permute-start(bf16[1,1,32,64]{3,2,1,0:T(8,128)(2,1)S(1)} %get-tuple-element.89), channel_id=1, source_target_pairs={{8,0},{16,8},{24,16},{32,24},{40,32},{48,40},{56,48},{64,56},{72,6... | collective-permute-start | bytes 12296 | tf_op jit(solution)/shard_map/ppermute | solution.py:26
  300.9 1.9 collective-permute-start.16
  302.8 7.7 %collective-permute-start.17 = (bf16[1,1,64,128]{2,1,3,0:T(2,128)(2,1)S(1)}, bf16[1,1,64,128]{2,1,3,0:T(2,128)(2,1)S(1)}, u32[]{:S(2)}, u32[]{:S(2)}) collective-permute-start(bf16[1,1,64,128]{2,1,3,0:T(2,128)(2,1)S(1)} %get-tuple-element.57), channel_id=1, source_target_pairs={{8,0},{16,8},{24,16},{32,24},{40,32},{48,40},{56,48},{64,56},{72,6... | collective-permute-start | bytes 49160 | tf_op jit(solution)/shard_map/ppermute | solution.py:26
  310.6 1.8 collective-permute-done.17
  314.4 25.5 %all-gather.3.cloned.1.call-done = bf16[8,1,65536]{2,1,0:T(2,128)(2,1)} async-done(((bf16[1,1,65536]{2,1,0:T(2,128)(2,1)}), bf16[8,1,65536]{2,1,0:T(2,128)(2,1)}) %all-gather.3.cloned.1.call-update) | async-done | bytes 1048592 | tf_op jit(solution)/shard_map/all_gather | solution.py:103
  339.9 2.9 fusion
  343.7 144.2 %psum.23 = f32[1,8]{1,0:T(1,128)S(1)} all-reduce(f32[1,8]{1,0:T(1,128)S(1)} %fusion), channel_id=1, replica_groups=mesh['grid'=64,'state'=8] {'grid'}, use_global_device_ids=true, to_apply=%region_8.9 | all-reduce | flops 8 | bytes 64 | tf_op jit(solution)/shard_map/psum | solution.py:106
  (131 shorter events, 28.5 us)
Async XLA Ops:
  7.2 332.7 %all-gather.3.cloned.1.call-start = ((), (), s32[]{:S(2)}) async-start(), calls=%async_computation | async-start | bytes 2359296 | tf_op jit(solution)/shard_map/all_gather | solution.py:103
  8.7 25.6 %collective-permute-start.1 = (f32[1,2,64,128]{3,2,1,0:T(8,128)S(1)}, f32[1,2,64,128]{3,2,1,0:T(8,128)S(1)}, u32[]{:S(2)}, u32[]{:S(2)}) collective-permute-start(f32[1,2,64,128]{3,2,1,0:T(8,128)S(1)} %get-tuple-element.63), channel_id=1, source_target_pairs={{0,8},{8,16},{16,24},{24,32},{32,40},{40,48},{48,56},{56,64},{64,7... | collective-permute-start | bytes 196616 | tf_op jit(solution)/shard_map/ppermute | solution.py:23
  12.5 23.6 %collective-permute-start = (f32[1,2,64,128]{3,2,1,0:T(8,128)}, f32[1,2,64,128]{3,2,1,0:T(8,128)S(1)}, u32[]{:S(2)}, u32[]{:S(2)}) collective-permute-start(f32[1,2,64,128]{3,2,1,0:T(8,128)} %get-tuple-element.64), channel_id=1, source_target_pairs={{8,0},{16,8},{24,16},{32,24},{40,32},{48,40},{56,48},{64,56},{72,6... | collective-permute-start | bytes 196616 | tf_op jit(solution)/shard_map/ppermute | solution.py:26
  30.5 2.8 copy-start.1
  30.5 3.8 copy-start
  36.1 4.8 copy-start.2
  36.1 4.8 copy-start.3
  188.0 9.5 %collective-permute-start.2 = (bf16[1,1,64,128]{2,1,3,0:T(2,128)(2,1)S(1)}, bf16[1,1,64,128]{2,1,3,0:T(2,128)(2,1)S(1)}, u32[]{:S(2)}, u32[]{:S(2)}) collective-permute-start(bf16[1,1,64,128]{2,1,3,0:T(2,128)(2,1)S(1)} %get-tuple-element.58), channel_id=1, source_target_pairs={{0,8},{8,16},{16,24},{24,32},{32,40},{40,48},{48,56},{56,64},{64,7... | collective-permute-start | bytes 49160 | tf_op jit(solution)/shard_map/ppermute | solution.py:23
  190.0 9.1 %collective-permute-start.3 = (bf16[1,1,64,128]{2,1,3,0:T(2,128)(2,1)S(1)}, bf16[1,1,64,128]{2,1,3,0:T(2,128)(2,1)S(1)}, u32[]{:S(2)}, u32[]{:S(2)}) collective-permute-start(bf16[1,1,64,128]{2,1,3,0:T(2,128)(2,1)S(1)} %get-tuple-element.59), channel_id=1, source_target_pairs={{8,0},{16,8},{24,16},{32,24},{40,32},{48,40},{56,48},{64,56},{72,6... | collective-permute-start | bytes 49160 | tf_op jit(solution)/shard_map/ppermute | solution.py:26
  225.4 9.5 %collective-permute-start.4 = (bf16[1,1,32,64]{3,2,1,0:T(8,128)(2,1)S(1)}, bf16[1,1,32,64]{3,2,1,0:T(8,128)(2,1)S(1)}, u32[]{:S(2)}, u32[]{:S(2)}) collective-permute-start(bf16[1,1,32,64]{3,2,1,0:T(8,128)(2,1)S(1)} %get-tuple-element.90), channel_id=1, source_target_pairs={{0,8},{8,16},{16,24},{24,32},{32,40},{40,48},{48,56},{56,64},{64,7... | collective-permute-start | bytes 12296 | tf_op jit(solution)/shard_map/ppermute | solution.py:23
  227.3 8.9 %collective-permute-start.5 = (bf16[1,1,32,64]{3,2,1,0:T(8,128)(2,1)S(1)}, bf16[1,1,32,64]{3,2,1,0:T(8,128)(2,1)S(1)}, u32[]{:S(2)}, u32[]{:S(2)}) collective-permute-start(bf16[1,1,32,64]{3,2,1,0:T(8,128)(2,1)S(1)} %get-tuple-element.91), channel_id=1, source_target_pairs={{8,0},{16,8},{24,16},{32,24},{40,32},{48,40},{56,48},{64,56},{72,6... | collective-permute-start | bytes 12296 | tf_op jit(solution)/shard_map/ppermute | solution.py:26
  239.0 9.5 %collective-permute-start.6 = (bf16[1,1,16,32]{3,2,1,0:T(8,128)(2,1)S(1)}, bf16[1,1,16,32]{3,2,1,0:T(8,128)(2,1)S(1)}, u32[]{:S(2)}, u32[]{:S(2)}) collective-permute-start(bf16[1,1,16,32]{3,2,1,0:T(8,128)(2,1)S(1)} %get-tuple-element.115), channel_id=1, source_target_pairs={{0,8},{8,16},{16,24},{24,32},{32,40},{40,48},{48,56},{56,64},{64,7... | collective-permute-start | bytes 3080 | tf_op jit(solution)/shard_map/ppermute | solution.py:23
  240.9 8.8 %collective-permute-start.7 = (bf16[1,1,16,32]{3,2,1,0:T(8,128)(2,1)S(1)}, bf16[1,1,16,32]{3,2,1,0:T(8,128)(2,1)S(1)}, u32[]{:S(2)}, u32[]{:S(2)}) collective-permute-start(bf16[1,1,16,32]{3,2,1,0:T(8,128)(2,1)S(1)} %get-tuple-element.116), channel_id=1, source_target_pairs={{8,0},{16,8},{24,16},{32,24},{40,32},{48,40},{56,48},{64,56},{72,6... | collective-permute-start | bytes 3080 | tf_op jit(solution)/shard_map/ppermute | solution.py:26
  250.2 9.4 %collective-permute-start.9 = (bf16[1,1,8,16]{3,2,1,0:T(8,128)(2,1)S(1)}, bf16[1,1,8,16]{3,2,1,0:T(8,128)(2,1)S(1)}, u32[]{:S(2)}, u32[]{:S(2)}) collective-permute-start(bf16[1,1,8,16]{3,2,1,0:T(8,128)(2,1)S(1)} %get-tuple-element.126), channel_id=1, source_target_pairs={{8,0},{16,8},{24,16},{32,24},{40,32},{48,40},{56,48},{64,56},{72,6... | collective-permute-start | bytes 776 | tf_op jit(solution)/shard_map/ppermute | solution.py:26
  257.7 8.8 %collective-permute-start.8 = (bf16[1,1,8,16]{3,2,1,0:T(8,128)(2,1)S(1)}, bf16[1,1,8,16]{3,2,1,0:T(8,128)(2,1)S(1)}, u32[]{:S(2)}, u32[]{:S(2)}) collective-permute-start(bf16[1,1,8,16]{3,2,1,0:T(8,128)(2,1)S(1)} %get-tuple-element.126), channel_id=1, source_target_pairs={{0,8},{8,16},{16,24},{24,32},{32,40},{40,48},{48,56},{56,64},{64,7... | collective-permute-start | bytes 776 | tf_op jit(solution)/shard_map/ppermute | solution.py:23
  266.7 5.9 %collective-permute-start.11 = (bf16[1,1,8,16]{3,2,1,0:T(8,128)(2,1)S(1)}, bf16[1,1,8,16]{3,2,1,0:T(8,128)(2,1)S(1)}, u32[]{:S(2)}, u32[]{:S(2)}) collective-permute-start(bf16[1,1,8,16]{3,2,1,0:T(8,128)(2,1)S(1)} %get-tuple-element.16), channel_id=1, source_target_pairs={{8,0},{16,8},{24,16},{32,24},{40,32},{48,40},{56,48},{64,56},{72,6... | collective-permute-start | bytes 776 | tf_op jit(solution)/shard_map/ppermute | solution.py:26
  268.7 8.8 %collective-permute-start.10 = (bf16[1,1,8,16]{3,2,1,0:T(8,128)(2,1)S(1)}, bf16[1,1,8,16]{3,2,1,0:T(8,128)(2,1)S(1)}, u32[]{:S(2)}, u32[]{:S(2)}) collective-permute-start(bf16[1,1,8,16]{3,2,1,0:T(8,128)(2,1)S(1)} %get-tuple-element.16), channel_id=1, source_target_pairs={{0,8},{8,16},{16,24},{24,32},{32,40},{40,48},{48,56},{56,64},{64,7... | collective-permute-start | bytes 776 | tf_op jit(solution)/shard_map/ppermute | solution.py:23
  277.9 9.2 %collective-permute-start.12 = (bf16[1,1,16,32]{3,2,1,0:T(8,128)(2,1)S(1)}, bf16[1,1,16,32]{3,2,1,0:T(8,128)(2,1)S(1)}, u32[]{:S(2)}, u32[]{:S(2)}) collective-permute-start(bf16[1,1,16,32]{3,2,1,0:T(8,128)(2,1)S(1)} %get-tuple-element.113), channel_id=1, source_target_pairs={{0,8},{8,16},{16,24},{24,32},{32,40},{40,48},{48,56},{56,64},{64,7... | collective-permute-start | bytes 3080 | tf_op jit(solution)/shard_map/ppermute | solution.py:23
  279.8 8.6 %collective-permute-start.13 = (bf16[1,1,16,32]{3,2,1,0:T(8,128)(2,1)S(1)}, bf16[1,1,16,32]{3,2,1,0:T(8,128)(2,1)S(1)}, u32[]{:S(2)}, u32[]{:S(2)}) collective-permute-start(bf16[1,1,16,32]{3,2,1,0:T(8,128)(2,1)S(1)} %get-tuple-element.114), channel_id=1, source_target_pairs={{8,0},{16,8},{24,16},{32,24},{40,32},{48,40},{56,48},{64,56},{72,6... | collective-permute-start | bytes 3080 | tf_op jit(solution)/shard_map/ppermute | solution.py:26
  289.0 9.6 %collective-permute-start.14 = (bf16[1,1,32,64]{3,2,1,0:T(8,128)(2,1)S(1)}, bf16[1,1,32,64]{3,2,1,0:T(8,128)(2,1)S(1)}, u32[]{:S(2)}, u32[]{:S(2)}) collective-permute-start(bf16[1,1,32,64]{3,2,1,0:T(8,128)(2,1)S(1)} %get-tuple-element.88), channel_id=1, source_target_pairs={{0,8},{8,16},{16,24},{24,32},{32,40},{40,48},{48,56},{56,64},{64,7... | collective-permute-start | bytes 12296 | tf_op jit(solution)/shard_map/ppermute | solution.py:23
  290.9 8.9 %collective-permute-start.15 = (bf16[1,1,32,64]{3,2,1,0:T(8,128)(2,1)S(1)}, bf16[1,1,32,64]{3,2,1,0:T(8,128)(2,1)S(1)}, u32[]{:S(2)}, u32[]{:S(2)}) collective-permute-start(bf16[1,1,32,64]{3,2,1,0:T(8,128)(2,1)S(1)} %get-tuple-element.89), channel_id=1, source_target_pairs={{8,0},{16,8},{24,16},{32,24},{40,32},{48,40},{56,48},{64,56},{72,6... | collective-permute-start | bytes 12296 | tf_op jit(solution)/shard_map/ppermute | solution.py:26
  300.9 9.8 %collective-permute-start.16 = (bf16[1,1,64,128]{2,1,3,0:T(2,128)(2,1)S(1)}, bf16[1,1,64,128]{2,1,3,0:T(2,128)(2,1)S(1)}, u32[]{:S(2)}, u32[]{:S(2)}) collective-permute-start(bf16[1,1,64,128]{2,1,3,0:T(2,128)(2,1)S(1)} %get-tuple-element.56), channel_id=1, source_target_pairs={{0,8},{8,16},{16,24},{24,32},{32,40},{40,48},{48,56},{56,64},{64,7... | collective-permute-start | bytes 49160 | tf_op jit(solution)/shard_map/ppermute | solution.py:23
  302.8 9.6 %collective-permute-start.17 = (bf16[1,1,64,128]{2,1,3,0:T(2,128)(2,1)S(1)}, bf16[1,1,64,128]{2,1,3,0:T(2,128)(2,1)S(1)}, u32[]{:S(2)}, u32[]{:S(2)}) collective-permute-start(bf16[1,1,64,128]{2,1,3,0:T(2,128)(2,1)S(1)} %get-tuple-element.57), channel_id=1, source_target_pairs={{8,0},{16,8},{24,16},{32,24},{40,32},{48,40},{56,48},{64,56},{72,6... | collective-permute-start | bytes 49160 | tf_op jit(solution)/shard_map/ppermute | solution.py:26
Sparse Core Ops, SparseCore 0:
  314.4 25.4 all-gather.2
where the time goes:
time: 496 us; the launch traced here: 495 us
  blocking collectives  285 us (57%)
  starting transfers between devices  87.3 us (18%)
  waiting for transfers between devices  46.1 us (9%)
  local copies, waits for them, and re-layouts  42.6 us (9%)
  between operations  16 us (3%)
  other arithmetic  15.5 us (3%)
    psum x1, blocking collectives, on_device(): summed = lax.psum(row_block, 'grid')  144 us
    psum x1, blocking collectives, on_device(): lax.psum((jnp.sum(orbitals * hpsi, axis=(1, 2, 3)), jnp.sum(orbitals * or...  141 us
    ppermute x9, starting transfers between devices, with_halo(): lax.ppermute(lax.slice_in_dim(block, 0, width, axis=dim), axis, backward)  66.1 us
    all_gather x1, waiting for transfers between devices, on_device(): lax.all_gather(rounded, 'state', axis=0, tiled=True)  25.5 us
    ppermute x9, starting transfers between devices, with_halo(): lax.ppermute(lax.slice_in_dim(block, block.shape[dim] - width, None, axis...  21.2 us
    reshape x2, local copies, waits for them, and re-layouts, restrict(): shaped = values.reshape(count, sx // 2, 2, sy // 2, 2, sz // 2, 2)  20.2 us
    ppermute x9, waiting for transfers between devices, with_halo(): lax.ppermute(lax.slice_in_dim(block, block.shape[dim] - width, None, axis...  12.1 us
  transfers between devices with their start and end apart: 19, of which 11 were waited for; matrix products, arithmetic and copies ran while one was open for 2% of the time, Pallas kernels for 0%

commit v1 on v0

v1 whole, which is shorter than its diff:
```python
import functools

import jax
import jax.numpy as jnp
from jax import lax
from jax.experimental import pallas as pl
from jax.experimental.pallas import tpu as pltpu
from jax.sharding import PartitionSpec as P

MESH = pl.DeviceIdType.MESH
HIGH = lax.Precision.HIGHEST
F32 = jnp.float32

SHIFT_TERM = 0.25
DAMPING = 2.0 / 3.0
LANES = 128
ROWS = 64
PLANES = 8
STATES = 8
RING = 16
REACH = 3


def scales(level):
    inverse = 0.25**level
    diagonal = SHIFT_TERM + 3.0 * inverse
    scaled = DAMPING / diagonal
    return scaled, 0.5 * inverse * scaled


def iota(shape, dim):
    return lax.broadcasted_iota(jnp.int32, shape, dim)


def beside(plane, segment):
    rows = plane.shape[0]
    total = pltpu.roll(plane, 1, 0) + pltpu.roll(plane, rows - 1, 0)
    low, high = pltpu.roll(plane, 1, 1), pltpu.roll(plane, LANES - 1, 1)
    if segment != LANES:
        cell = iota(plane.shape, 1) & (segment - 1)
        low = jnp.where(cell == 0, pltpu.roll(plane, LANES - segment + 1, 1), low)
        high = jnp.where(cell == segment - 1, pltpu.roll(plane, segment - 1, 1), high)
    return total + (low + high)


def beside_two(plane):
    rows = plane.shape[0]
    total = pltpu.roll(plane, 2, 0) + pltpu.roll(plane, rows - 2, 0)
    return total + (pltpu.roll(plane, 2, 1) + pltpu.roll(plane, LANES - 2, 1))


def matrices():
    k, j = iota((LANES, LANES), 0), iota((LANES, LANES), 1)
    down_h = (j < 64) & ((k >> 1) == j)
    down_o = (j >= 64) & ((k >> 1) == j - 64)
    down_two = ((k >> 6) == ((j >> 5) & 1)) & (((k & 63) >> 1) == (j & 31))
    down_three = (k < 64) & ((k >> 5) == ((j >> 4) & 1)) & (((k & 31) >> 1) == (j & 15))
    up_two = (k < 32) & ((k >> 4) == ((j >> 5) & 1)) & ((k & 15) == ((j & 31) >> 1))
    up_one = (k < 64) & ((k >> 5) == (j >> 6)) & ((k & 31) == ((j & 63) >> 1))
    up_zero = k == (j >> 1)
    eighth, one = jnp.full((LANES, LANES), 0.125, F32), jnp.ones((LANES, LANES), F32)
    zero = jnp.zeros((LANES, LANES), F32)
    return [
        jnp.where(mask, eighth, zero) for mask in (down_h, down_o, down_two, down_three)
    ] + [jnp.where(mask, one, zero) for mask in (up_two, up_one, up_zero)]


def times(left, right):
    return jnp.dot(left, right, precision=HIGH, preferred_element_type=F32)


def kernel(
    slabs,
    o_hbm, p_hbm, out_ref, gram_ref,
    o_buf, p_buf, h_buf, pair_buf, mats, f1_buf, f2_buf, f3_buf, two_buf, three_buf,
    up2_buf, up1_buf, up0_buf, e_y, e_z, rounded, mixed, rows_buf, g_z, g_xy,
    load_sem, halo_send, halo_recv, f1_send, f1_recv, f23_send, f23_recv,
    ey_send, ey_recv, ez_send, ez_recv, x_send, x_recv, gz_send, gz_recv, gx_send, gx_recv,
):
    g, s = lax.axis_index("grid"), lax.axis_index("state")
    y, z = g // RING, g % RING
    columns = slabs // RING

    def slab(step):
        return (lax.rem(g + step + slabs, slabs), s)

    def on_ring(step):
        return (y * RING + lax.rem(z + step, RING), s)

    def on_column(step):
        return (lax.rem(y + step, columns) * RING + z, s)

    def on_face(step):
        up, side = step // STATES, step % STATES
        return (lax.rem(y + up, columns) * RING + z, lax.rem(s + side, STATES))

    def send(src, dst, send_sem, recv_sem, peer):
        return pltpu.make_async_remote_copy(
            src_ref=src, dst_ref=dst, send_sem=send_sem, recv_sem=recv_sem,
            device_id=peer, device_id_type=MESH,
        )

    loads = [
        pltpu.make_async_copy(o_hbm.at[0], o_buf.at[pl.ds(3, PLANES)], load_sem.at[0]),
        pltpu.make_async_copy(p_hbm, p_buf.at[pl.ds(1, PLANES)], load_sem.at[1]),
    ]
    for load in loads:
        load.start()

    peers = [slab(d) for step in range(1, REACH + 1) for d in (step, -step)]
    peers += [on_ring(d) for d in range(1, RING)]
    peers += [on_face(d) for d in range(1, STATES * columns)]
    barrier = pltpu.get_barrier_semaphore()
    for peer in peers:
        pl.semaphore_signal(barrier, inc=1, device_id=peer, device_id_type=MESH)
    pl.semaphore_wait(barrier, len(peers))

    halos = [
        send(o_hbm.at[0, pl.ds(5, 3)], o_buf.at[pl.ds(0, 3)], halo_send.at[0], halo_recv.at[0], slab(1)),
        send(o_hbm.at[0, pl.ds(0, 3)], o_buf.at[pl.ds(11, 3)], halo_send.at[1], halo_recv.at[1], slab(-1)),
        send(p_hbm.at[pl.ds(7, 1)], p_buf.at[pl.ds(0, 1)], halo_send.at[2], halo_recv.at[2], slab(1)),
        send(p_hbm.at[pl.ds(0, 1)], p_buf.at[pl.ds(9, 1)], halo_send.at[3], halo_recv.at[3], slab(-1)),
    ]
    for copy in halos:
        copy.start()
    for index, matrix in enumerate(matrices()):
        mats[index] = matrix
    rows_buf[...] = jnp.zeros_like(rows_buf)
    for load in loads:
        load.wait()

    c0, k0 = scales(0)
    near = {}

    def apply_h(p):
        centre = o_buf[p + 3]
        first = (o_buf[p + 2] + o_buf[p + 4]) + beside(centre, LANES)
        second = (o_buf[p + 1] + o_buf[p + 5]) + beside_two(centre)
        value = (3.75 + p_buf[p + 1]) * centre - (2.0 / 3.0) * first + (1.0 / 24.0) * second
        h_buf[p + 1] = value
        if 0 <= p < PLANES:
            up0_buf[p] = centre * (1.0 / 3.0) + k0 * first
        return value

    for p in range(2, PLANES - 2):
        apply_h(p)
    for copy in halos:
        copy.wait()
    for p in (-1, 0, 1, PLANES - 2, PLANES - 1, PLANES):
        apply_h(p)

    top = jnp.zeros((ROWS, LANES), F32)
    bottom = jnp.zeros((ROWS, LANES), F32)
    for p in range(PLANES):
        centre = o_buf[p + 3]
        top += centre * h_buf[p + 1]
        bottom += centre * centre
    top, bottom = jnp.sum(top, 0, keepdims=True), jnp.sum(bottom, 0, keepdims=True)
    lane_row = iota((1, LANES), 1)
    e_y[y] = jnp.where(
        lane_row < 64, top + pltpu.roll(top, 64, 1), bottom + pltpu.roll(bottom, 64, 1)
    )
    energy_y = [
        send(e_y.at[y], e_y.at[y], ey_send.at[d - 1], ey_recv.at[d - 1], on_column(d))
        for d in range(1, columns)
    ]
    for copy in energy_y:
        copy.start()

    for q in range(PLANES // 2):
        both_h = None
        for p in (2 * q, 2 * q + 1):
            value = h_buf[p + 1]
            around = (h_buf[p] + h_buf[p + 2]) + beside(value, LANES)
            rest = value * (1.0 / 3.0) + k0 * around
            both_h = rest if both_h is None else both_h + rest
        pair_buf[q] = both_h
        pair_buf[q + 4] = up0_buf[2 * q] + up0_buf[2 * q + 1]
    halved = pair_buf[:, pl.ds(0, 32, 2), :] + pair_buf[:, pl.ds(1, 32, 2), :]
    f1 = times(halved[:4].reshape(LANES, LANES), mats[0]) + times(
        halved[4:].reshape(LANES, LANES), mats[1]
    )
    f1_buf[3:7] = f1.reshape(4, 32, LANES)
    first = [
        send(f1_buf.at[pl.ds(4, 3)], f1_buf.at[pl.ds(0, 3)], f1_send.at[0], f1_recv.at[0], slab(1)),
        send(f1_buf.at[pl.ds(3, 3)], f1_buf.at[pl.ds(7, 3)], f1_send.at[1], f1_recv.at[1], slab(-1)),
    ]
    for copy in first:
        copy.start()

    for copy in energy_y:
        copy.wait()
    e_z[z] = jnp.sum(e_y[...], axis=0)
    energy_z = [
        send(e_z.at[z], e_z.at[z], ez_send.at[d - 1], ez_recv.at[d - 1], on_ring(d))
        for d in range(1, RING)
    ]
    for copy in energy_z:
        copy.start()
    for copy in first:
        copy.wait()

    c1, k1 = scales(1)
    c2, k2 = scales(2)
    c3, k3 = scales(3)

    def remainder(buf, index, factor, segment):
        plane = buf[index]
        around = (buf[index - 1] + buf[index + 1]) + beside(plane, segment)
        return plane * (1.0 / 3.0) + factor * around

    for q in range(4):
        two_buf[q] = remainder(f1_buf, 2 * q + 1, k1, 64) + remainder(f1_buf, 2 * q + 2, k1, 64)
    halved = two_buf[:, pl.ds(0, 16, 2), :] + two_buf[:, pl.ds(1, 16, 2), :]
    f2_buf[1:5] = times(halved.reshape(64, LANES), mats[2]).reshape(4, 16, LANES)
    second = [
        send(f2_buf.at[3], f2_buf.at[5], f23_send.at[0], f23_recv.at[0], slab(-1)),
        send(f2_buf.at[2], f2_buf.at[0], f23_send.at[1], f23_recv.at[1], slab(1)),
    ]
    three_buf[...] = remainder(f2_buf, 2, k2, 32) + remainder(f2_buf, 3, k2, 32)
    halved = three_buf[pl.ds(0, 8, 2), :] + three_buf[pl.ds(1, 8, 2), :]
    f3_buf[REACH] = times(halved, mats[3])
    third = []
    for d in range(1, REACH + 1):
        for step in (d, -d):
            at = len(third) + 2
            third.append(
                send(f3_buf.at[REACH], f3_buf.at[REACH - step], f23_send.at[at], f23_recv.at[at], slab(step))
            )
    for copy in third[::-1] + second:
        copy.start()
    for copy in second + third:
        copy.wait()

    source = {p: f3_buf[p + REACH] for p in range(-REACH, REACH + 1)}
    iterate = {p: c3 * source[p] for p in source}
    for reach in (REACH - 1, REACH - 2):
        iterate = {
            p: iterate[p] * (1.0 / 3.0) + c3 * source[p]
            + k3 * ((iterate[p - 1] + iterate[p + 1]) + beside(iterate[p], 16))
            for p in range(-reach, reach + 1)
        }
    for p in range(-1, 2):
        spread = times(iterate[p], mats[4])
        up2_buf[p + 1, pl.ds(0, 8, 2), :] = spread
        up2_buf[p + 1, pl.ds(1, 8, 2), :] = spread
    fixed = {p: c2 * f2_buf[p + 2] + up2_buf[(p >> 1) + 1] for p in range(-2, 4)}
    for p in range(-1, 3):
        value = (
            fixed[p] * (1.0 / 3.0) + c2 * f2_buf[p + 2]
            + k2 * ((fixed[p - 1] + fixed[p + 1]) + beside(fixed[p], 32))
        )
        spread = times(value, mats[5])
        up1_buf[p + 1, pl.ds(0, 16, 2), :] = spread
        up1_buf[p + 1, pl.ds(1, 16, 2), :] = spread
    fixed = {p: c1 * f1_buf[p + 3] + up1_buf[(p >> 1) + 1] for p in range(-2, 6)}
    error = {
        p: fixed[p] * (1.0 / 3.0) + c1 * f1_buf[p + 3]
        + k1 * ((fixed[p - 1] + fixed[p + 1]) + beside(fixed[p], 64))
        for p in range(-1, 5)
    }

    for copy in energy_z:
        copy.wait()
    sums = jnp.sum(e_z[...], axis=0)
    numer = jnp.sum(jnp.where(lane_row < 64, sums, 0.0), axis=1, keepdims=True)
    denom = jnp.sum(jnp.where(lane_row < 64, 0.0, sums), axis=1, keepdims=True)
    energy = numer / denom
    for p in range(-1, 5):
        spread = times(error[p] - energy * pltpu.roll(error[p], 64, 1), mats[6])
        up0_buf[p + 1, pl.ds(0, 32, 2), :] = spread
        up0_buf[p + 1, pl.ds(1, 32, 2), :] = spread
    for p in range(-1, PLANES + 1):
        residual = h_buf[p + 1] - energy * o_buf[p + 3]
        h_buf[p + 1] = residual
        p_buf[p + 1] = c0 * residual + up0_buf[(p >> 1) + 1]
    for p in range(PLANES):
        value = p_buf[p + 1]
        around = (p_buf[p] + p_buf[p + 2]) + beside(value, LANES)
        value = value * (1.0 / 3.0) + c0 * h_buf[p + 1] + k0 * around
        out_ref[0, p] = value
        rounded[p] = value.astype(jnp.bfloat16)
    mix = []
    for d in range(1, STATES):
        to = lax.rem(s + d, STATES)
        mix.append(send(rounded.at[to], mixed.at[s], x_send.at[d - 1], x_recv.at[d - 1], (g, to)))
    for copy in mix:
        copy.start()
    mixed[s] = rounded[s]
    for copy in mix:
        copy.wait()

    pairs = [(i, j) for i in range(STATES) for j in range(i, STATES)]
    held = {pair: None for pair in pairs}
    for block in range(ROWS // 16):
        values = [mixed[i, 16 * block : 16 * block + 16].astype(F32) for i in range(STATES)]
        for i, j in pairs:
            product = values[i] * values[j]
            product = product[:8] + product[8:]
            held[i, j] = product if held[i, j] is None else held[i, j] + product
    for i, j in pairs:
        row = jnp.sum(held[i, j], 0, keepdims=True)
        rows_buf[8 * i + j : 8 * i + j + 1] = row
        if i != j:
            rows_buf[8 * j + i : 8 * j + i + 1] = row
    flat = lax.dot_general(
        jnp.ones((8, LANES), F32), rows_buf[...], (((1,), (1,)), ((), ())),
        precision=HIGH, preferred_element_type=F32,
    )
    g_z[z] = flat[:1]
    gram_z = [
        send(g_z.at[z], g_z.at[z], gz_send.at[d - 1], gz_recv.at[d - 1], on_ring(d))
        for d in range(1, RING)
    ]
    for copy in gram_z:
        copy.start()
    for copy in gram_z:
        copy.wait()
    mine = y * STATES + s
    g_xy[mine] = jnp.sum(g_z[...], axis=0)
    gram_xy = [
        send(g_xy.at[mine], g_xy.at[mine], gx_send.at[d - 1], gx_recv.at[d - 1], on_face(d))
        for d in range(1, STATES * columns)
    ]
    for copy in gram_xy:
        copy.start()
    for copy in gram_xy:
        copy.wait()
    total = jnp.sum(g_xy[...], axis=0)
    picked = jnp.zeros((1, STATES), F32)
    for t in range(STATES):
        picked += jnp.where(s == t, total[:, STATES * t : STATES * t + STATES], 0.0)
    gram_ref[...] = picked / F32(PLANES * ROWS * LANES * slabs)


def solution(mesh):
    slabs = mesh.shape["grid"]
    columns = slabs // RING
    faces = STATES * columns
    dma = pltpu.SemaphoreType.DMA

    def on_device(orbitals, potential):
        return pl.pallas_call(
            functools.partial(kernel, slabs),
            out_shape=(
                jax.ShapeDtypeStruct((1, PLANES, ROWS, LANES), F32),
                jax.ShapeDtypeStruct((1, STATES), F32),
            ),
            in_specs=[pl.BlockSpec(memory_space=pl.ANY)] * 2,
            out_specs=(
                pl.BlockSpec(memory_space=pltpu.VMEM),
                pl.BlockSpec(memory_space=pltpu.VMEM),
            ),
            scratch_shapes=[
                pltpu.VMEM((PLANES + 6, ROWS, LANES), F32),
                pltpu.VMEM((PLANES + 2, ROWS, LANES), F32),
                pltpu.VMEM((PLANES + 2, ROWS, LANES), F32),
                pltpu.VMEM((8, ROWS, LANES), F32),
                pltpu.VMEM((7, LANES, LANES), F32),
                pltpu.VMEM((10, 32, LANES), F32),
                pltpu.VMEM((6, 16, LANES), F32),
                pltpu.VMEM((2 * REACH + 1, 8, LANES), F32),
                pltpu.VMEM((4, 32, LANES), F32),
                pltpu.VMEM((16, LANES), F32),
                pltpu.VMEM((3, 16, LANES), F32),
                pltpu.VMEM((4, 32, LANES), F32),
                pltpu.VMEM((8, ROWS, LANES), F32),
                pltpu.VMEM((columns, 1, LANES), F32),
                pltpu.VMEM((RING, 1, LANES), F32),
                pltpu.VMEM((PLANES, ROWS, LANES), jnp.bfloat16),
                pltpu.VMEM((STATES, ROWS, LANES), jnp.bfloat16),
                pltpu.VMEM((LANES, LANES), F32),
                pltpu.VMEM((RING, 1, LANES), F32),
                pltpu.VMEM((faces, 1, LANES), F32),
                dma((2,)), dma((4,)), dma((4,)), dma((2,)), dma((2,)), dma((8,)), dma((8,)),
                dma((columns - 1,)), dma((columns - 1,)), dma((RING - 1,)), dma((RING - 1,)),
                dma((STATES - 1,)), dma((STATES - 1,)), dma((RING - 1,)), dma((RING - 1,)),
                dma((faces - 1,)), dma((faces - 1,)),
            ],
            compiler_params=pltpu.CompilerParams(
                collective_id=0, has_side_effects=True, vmem_limit_bytes=32 * 1024 * 1024
            ),
        )(orbitals, potential)

    return jax.shard_map(
        on_device,
        mesh=mesh,
        in_specs=(P("state", "grid", None, None), P("grid", None, None)),
        out_specs=(P("state", "grid", None, None), P("state", None)),
        check_vma=False,
    )
```

time: 496 us -> 55.2 us (0.11)
  the two profiles are of different devices: /device:TPU:2 before, /device:TPU:1 now
where the time goes in v1:
time: 55.2 us; the launch traced here: 55.1 us
  Pallas kernels  51.3 us (93%)
  local copies, waits for them, and re-layouts  3.11 us (6%)
  between operations  0.65 us (1%)
    pallas_call x1, Pallas kernels, on_device(): pl.pallas_call(functools.partial(kernel, slabs), out_shape=(jax.ShapeDtyp...  51.3 us
    unnamed x6, local copies, waits for them, and re-layouts  3.11 us

profile of v1, /device:TPU:1, one launch (start us, length us, event | category | flops | bytes accessed | tf_op | source)
XLA Modules:
  0.0 55.1 jit_solution(17849165826847922826)
XLA Ops:
  0.6 0.0 copy-start
  0.6 0.9 %copy-done = f32[1,8,64,128]{3,2,1,0:T(8,128)S(1)} copy-done((f32[1,8,64,128]{3,2,1,0:T(8,128)S(1)}, f32[1,8,64,128]{3,2,1,0:T(8,128)}, u32[]{:S(2)}) %copy-start) | copy-done | bytes 262168
  1.6 0.0 copy-start.1
  1.6 0.9 %copy-done.1 = f32[8,64,128]{2,1,0:T(8,128)S(1)} copy-done((f32[8,64,128]{2,1,0:T(8,128)S(1)}, f32[8,64,128]{2,1,0:T(8,128)}, u32[]{:S(2)}) %copy-start.1) | copy-done | bytes 262168
  2.5 51.3 %shard_map.41 = (f32[1,8,64,128]{3,2,1,0:T(8,128)S(1)}, f32[1,8]{1,0:T(1,128)S(1)}) custom-call(f32[1,8,64,128]{3,2,1,0:T(8,128)S(1)} %copy-done, f32[8,64,128]{2,1,0:T(8,128)S(1)} %copy-done.1), custom_call_target="tpu_custom_call" | custom-call | tf_op jit(solution)/shard_map/pallas_call | solution.py:343
  53.8 0.7 %copy.6 = f32[1,8,64,128]{3,2,1,0:T(8,128)} copy(f32[1,8,64,128]{3,2,1,0:T(8,128)S(1)} %get-tuple-element.4) | data formatting | bytes 524288
  54.5 0.5 copy.7
Async XLA Ops:
  0.6 1.0 %copy-start = (f32[1,8,64,128]{3,2,1,0:T(8,128)S(1)}, f32[1,8,64,128]{3,2,1,0:T(8,128)}, u32[]{:S(2)}) copy-start(f32[1,8,64,128]{3,2,1,0:T(8,128)} %o_hbm.1) | copy-start | bytes 786436
  1.6 0.9 %copy-start.1 = (f32[8,64,128]{2,1,0:T(8,128)S(1)}, f32[8,64,128]{2,1,0:T(8,128)}, u32[]{:S(2)}) copy-start(f32[8,64,128]{2,1,0:T(8,128)} %p_hbm.1) | copy-start | bytes 786436

commit v2 on v1

v2 whole, which is shorter than its diff:
```python
import functools

import jax
import jax.numpy as jnp
from jax import lax
from jax.experimental import pallas as pl
from jax.experimental.pallas import tpu as pltpu
from jax.sharding import PartitionSpec as P

MESH = pl.DeviceIdType.MESH
HIGH = lax.Precision.HIGHEST
F32 = jnp.float32

SHIFT_TERM = 0.25
DAMPING = 2.0 / 3.0
LANES = 128
ROWS = 64
HALF = ROWS // 2
PLANES = 8
STATES = 8
CHIPS = 4
RING = 16
REACH = 4
THIRD = 1.0 / 3.0
NEAR = -2.0 / 3.0
FAR = 1.0 / 24.0


def scales(level):
    inverse = 0.25**level
    diagonal = SHIFT_TERM + 3.0 * inverse
    scaled = DAMPING / diagonal
    return scaled, 0.5 * inverse * scaled


C0, K0 = scales(0)
C1, K1 = scales(1)
C2, K2 = scales(2)
C3, K3 = scales(3)


def iota(shape, dim):
    return lax.broadcasted_iota(jnp.int32, shape, dim)


def beside(plane, segment=LANES):
    rows = plane.shape[0]
    total = pltpu.roll(plane, 1, 0) + pltpu.roll(plane, rows - 1, 0)
    low, high = pltpu.roll(plane, 1, 1), pltpu.roll(plane, LANES - 1, 1)
    if segment != LANES:
        cell = iota(plane.shape, 1) & (segment - 1)
        low = jnp.where(cell == 0, pltpu.roll(plane, LANES - segment + 1, 1), low)
        high = jnp.where(cell == segment - 1, pltpu.roll(plane, segment - 1, 1), high)
    return total + (low + high)


def beside_two(plane):
    rows = plane.shape[0]
    total = pltpu.roll(plane, 2, 0) + pltpu.roll(plane, rows - 2, 0)
    return total + (pltpu.roll(plane, 2, 1) + pltpu.roll(plane, LANES - 2, 1))


def matrices():
    k, j = iota((LANES, LANES), 0), iota((LANES, LANES), 1)
    down_h = (j < 64) & ((k >> 1) == j)
    down_o = (j >= 64) & ((k >> 1) == j - 64)
    down_two = ((k >> 6) == ((j >> 5) & 1)) & (((k & 63) >> 1) == (j & 31))
    down_three = (k < 64) & ((k >> 5) == ((j >> 4) & 1)) & (((k & 31) >> 1) == (j & 15))
    up_two = (k < 32) & ((k >> 4) == ((j >> 5) & 1)) & ((k & 15) == ((j & 31) >> 1))
    up_one = (k < 64) & ((k >> 5) == (j >> 6)) & ((k & 31) == ((j & 63) >> 1))
    up_h = k == (j >> 1)
    up_o = k - 64 == (j >> 1)
    eighth, one = jnp.full((LANES, LANES), 0.125, F32), jnp.ones((LANES, LANES), F32)
    zero = jnp.zeros((LANES, LANES), F32)
    return [
        jnp.where(mask, eighth, zero) for mask in (down_h, down_o, down_two, down_three)
    ] + [jnp.where(mask, one, zero) for mask in (up_two, up_one, up_h, up_o)]


def times(left, right):
    return jnp.dot(left, right, precision=HIGH, preferred_element_type=F32)


def kernel(
    slabs,
    o_hbm, p_hbm, out_ref, gram_ref,
    o_buf, p_buf, h_buf, r_buf, g_out, g_in, pair_buf, mats,
    f1_buf, two_buf, f2_out, f2_in, three_buf, f3_in,
    up2_buf, up1_buf, uph_buf, upo_buf, a_buf, b_buf,
    e_y, e_z, rounded, mixed, rows_buf, g_z, g_xy,
    load_sem, halo_send, halo_recv, f1_sem, f2_sem, f3_sem, ey_sem, ez_sem, x_sem, gz_sem, gx_sem,
    token,
):
    g, s = lax.axis_index("grid"), lax.axis_index("state")
    y, z = g // RING, g % RING
    x, core = s // 2, s % 2
    columns = slabs // RING

    def slab(step):
        return (lax.rem(g + step + slabs, slabs), s)

    def on_ring(step):
        return (y * RING + lax.rem(z + step + RING, RING), s)

    def on_column(step):
        return (lax.rem(y + step + columns, columns) * RING + z, s)

    def state_at(step, other):
        return 2 * lax.rem(x + step + CHIPS, CHIPS) + (lax.rem(core + 1, 2) if other else core)

    def on_face(step):
        up, side = step // STATES, step % STATES
        return (lax.rem(y + up, columns) * RING + z, lax.rem(s + side, STATES))

    def send(src, dst, sems, peer):
        copy = pltpu.make_async_remote_copy(
            src_ref=src, dst_ref=dst, send_sem=sems[0], recv_sem=sems[1],
            device_id=peer, device_id_type=MESH,
        )
        copy.start()

    def take(sem, view):
        pltpu.make_async_copy(view, view, sem).wait()

    def signal(sem, peers):
        for peer in peers:
            pl.semaphore_signal(sem, inc=1, device_id=peer, device_id_type=MESH)

    partner = (g, state_at(0, True))
    close = [slab(1), slab(-1), on_ring(1), on_ring(-1), on_column(1), on_column(-1)]
    close += [(g, state_at(1, False)), (g, state_at(-1, False))]
    barrier = pltpu.get_barrier_semaphore()
    signal(barrier, close + [partner])
    loads = [
        pltpu.make_async_copy(o_hbm.at[0], o_buf.at[pl.ds(2, PLANES)], load_sem.at[0]),
        pltpu.make_async_copy(p_hbm, p_buf, load_sem.at[1]),
    ]
    for load in loads:
        load.start()
    with jax.named_scope("w_barrier"):
        pl.semaphore_wait(barrier, len(close) + 1)

    right, left = slab(1), slab(-1)

    def halo(part, mine, theirs):
        sems = (halo_send, halo_recv.at[part])
        send(o_hbm.at[0, pl.ds(6, 2), pl.ds(mine, HALF)], o_buf.at[pl.ds(0, 2), pl.ds(mine, HALF)], sems, right)
        send(o_hbm.at[0, pl.ds(0, 2), pl.ds(theirs, HALF)], o_buf.at[pl.ds(10, 2), pl.ds(theirs, HALF)], sems, left)

    signal(token.at[0], close)
    halo(0, 0, HALF)
    with jax.named_scope("w_load"):
        for load in loads:
            load.wait()
    g_out[0] = p_buf[0] * o_buf[2] + FAR * o_buf[4]
    g_out[1] = p_buf[7] * o_buf[9] + FAR * o_buf[7]
    with jax.named_scope("w_t1"):
        pl.semaphore_wait(token.at[0], len(close))
    signal(token.at[1], [slab(2), slab(-2), on_ring(2), on_ring(-2)])
    halo(1, HALF, 0)
    sems = (halo_send, halo_recv.at[2])
    send(g_out.at[1], g_in.at[0], sems, right)
    send(g_out.at[0], g_in.at[1], sems, left)

    top = jnp.zeros((ROWS, LANES), F32)
    bottom = jnp.zeros((ROWS, LANES), F32)
    for p in range(PLANES):
        centre = o_buf[p + 2]
        first, second = beside(centre), beside_two(centre)
        for q in (p - 1, p + 1):
            if 0 <= q < PLANES:
                first += o_buf[q + 2]
        for q in (p - 2, p + 2):
            if 0 <= q < PLANES:
                second += o_buf[q + 2]
        value = (3.75 + p_buf[p]) * centre + NEAR * first + FAR * second
        h_buf[p + 1] = value
        r_buf[p] = centre * THIRD + K0 * first
        top += centre * value
        bottom += centre * centre
    for index, matrix in enumerate(matrices()):
        mats[index] = matrix
    rows_buf[...] = jnp.zeros_like(rows_buf)
    top, bottom = jnp.sum(top, 0, keepdims=True), jnp.sum(bottom, 0, keepdims=True)
    lane_row = iota((1, LANES), 1)
    with jax.named_scope("w_t2"):
        pl.semaphore_wait(token.at[1], 4)
    signal(token.at[2], [on_ring(4), on_ring(-4), partner])

    with jax.named_scope("w_halo_a"):
        take(halo_recv.at[0], o_buf.at[pl.ds(0, 2)])
    cross = o_buf[2, :HALF] * (2.0 * NEAR * o_buf[1, :HALF] + 2.0 * FAR * o_buf[0, :HALF])
    cross += 2.0 * FAR * o_buf[1, :HALF] * o_buf[3, :HALF]
    cross += o_buf[9, HALF:] * (2.0 * NEAR * o_buf[10, HALF:] + 2.0 * FAR * o_buf[11, HALF:])
    cross += 2.0 * FAR * o_buf[10, HALF:] * o_buf[8, HALF:]
    top += jnp.sum(cross, 0, keepdims=True)
    e_y[y] = jnp.where(
        lane_row < 64, top + pltpu.roll(top, 64, 1), bottom + pltpu.roll(bottom, 64, 1)
    )
    for d in range(1, columns):
        send(e_y.at[y], e_y.at[y], (ey_sem.at[0], ey_sem.at[1]), on_column(d))

    with jax.named_scope("w_halo_b"):
        take(halo_recv.at[1], o_buf.at[pl.ds(0, 2)])
        take(halo_recv.at[2], g_in)
    h_buf[1] += NEAR * o_buf[1] + FAR * o_buf[0]
    h_buf[2] += FAR * o_buf[1]
    h_buf[8] += NEAR * o_buf[10] + FAR * o_buf[11]
    h_buf[7] += FAR * o_buf[10]
    r_buf[0] += K0 * o_buf[1]
    r_buf[7] += K0 * o_buf[10]
    for ghost, at, inner, outer, side in ((1, 0, 2, 0, 0), (10, 9, 9, 11, 1)):
        centre = o_buf[ghost]
        first = (o_buf[inner] + o_buf[outer]) + beside(centre)
        second = o_buf[2 * inner - ghost] + beside_two(centre)
        h_buf[at] = 3.75 * centre + g_in[side] + NEAR * first + FAR * second
    for q in range(PLANES // 2):
        both = None
        for p in (2 * q, 2 * q + 1):
            value = h_buf[p + 1]
            rest = value * THIRD + K0 * ((h_buf[p] + h_buf[p + 2]) + beside(value))
            both = rest if both is None else both + rest
        pair_buf[q] = both
        pair_buf[q + 4] = r_buf[2 * q] + r_buf[2 * q + 1]
    halved = pair_buf[:, pl.ds(0, 32, 2), :] + pair_buf[:, pl.ds(1, 32, 2), :]
    f1 = times(halved[:4].reshape(LANES, LANES), mats[0]) + times(
        halved[4:].reshape(LANES, LANES), mats[1]
    )
    f1 = f1.reshape(4, 32, LANES)
    f1_buf[2:6] = f1

    rest = []
    for p in range(4):
        total = beside(f1[p], 64)
        for q in (p - 1, p + 1):
            if 0 <= q < 4:
                total += f1[q]
        rest.append(f1[p] * THIRD + K1 * total)
    two_buf[0] = K1 * f1[0]
    two_buf[1] = rest[0] + rest[1]
    two_buf[2] = rest[2] + rest[3]
    two_buf[3] = K1 * f1[3]
    halved = two_buf[:, pl.ds(0, 16, 2), :] + two_buf[:, pl.ds(1, 16, 2), :]
    share = times(halved.reshape(64, LANES), mats[2]).reshape(4, 16, LANES)
    low = iota((16, LANES), 1) < 64
    f2_out[0] = jnp.where(low, share[0], share[1])
    f2_out[1] = jnp.where(low, share[2], share[3])
    a, b, c, d = share[0], share[1], share[2], share[3]
    three_buf[0] = a * (K2 + THIRD) + K2 * (b + beside(a, 32))
    three_buf[1] = (b + c) * (THIRD + K2) + K2 * ((a + d) + (beside(b, 32) + beside(c, 32)))
    three_buf[2] = d * (K2 + THIRD) + K2 * (c + beside(d, 32))
    halved = three_buf[:, pl.ds(0, 8, 2), :] + three_buf[:, pl.ds(1, 8, 2), :]
    parts = times(halved.reshape(24, LANES), mats[3]).reshape(3, 8, LANES)
    lane = iota((8, LANES), 1)
    f3_in[REACH] = jnp.where(
        lane < 32, parts[0],
        jnp.where(lane < 64, parts[1], jnp.where(lane < 96, parts[2], 0.0)),
    )
    sems = (f3_sem.at[0], f3_sem.at[1])
    for step in range(REACH, 0, -1):
        send(f3_in.at[REACH], f3_in.at[REACH - step], sems, slab(step))
        send(f3_in.at[REACH], f3_in.at[REACH + step], sems, slab(-step))

    with jax.named_scope("w_ey"):
        take(ey_sem.at[1], e_y.at[pl.ds(0, columns - 1)])
    e_z[z] = jnp.sum(e_y[...], axis=0)
    with jax.named_scope("w_t3"):
        pl.semaphore_wait(token.at[2], 3)
    for d in range(1, RING):
        send(e_z.at[z], e_z.at[z], (ez_sem.at[0], ez_sem.at[1]), on_ring(d))
    sems = (f2_sem.at[0], f2_sem.at[1])
    send(f2_out, f2_in.at[pl.ds(0, 2)], sems, right)
    send(f2_out, f2_in.at[pl.ds(2, 2)], sems, left)
    send(f2_out.at[1], f2_in.at[4], sems, slab(2))
    send(f2_out.at[0], f2_in.at[5], sems, slab(-2))
    sems = (f1_sem.at[0], f1_sem.at[1])
    send(f1_buf.at[pl.ds(4, 2)], f1_buf.at[pl.ds(0, 2)], sems, right)
    send(f1_buf.at[pl.ds(2, 2)], f1_buf.at[pl.ds(6, 2)], sems, left)

    with jax.named_scope("w_f"):
        take(f3_sem.at[1], f3_in.at[pl.ds(0, 2 * REACH)])
        take(f2_sem.at[1], f2_in)
        take(f1_sem.at[1], f1_buf.at[pl.ds(0, 4)])

    source = {}
    for p in range(1 - REACH, REACH):
        at = p + REACH
        total = jnp.where(lane < 32, f3_in[at + 1], jnp.where(lane < 64, f3_in[at], f3_in[at - 1]))
        total = total + pltpu.roll(total, 32, 1)
        source[p] = total + pltpu.roll(total, 64, 1)
    iterate = {p: C3 * source[p] for p in source}
    for reach in (2, 1):
        iterate = {
            p: iterate[p] * THIRD + C3 * source[p]
            + K3 * ((iterate[p - 1] + iterate[p + 1]) + beside(iterate[p], 16))
            for p in range(-reach, reach + 1)
        }
    spread = times(jnp.concatenate([iterate[p] for p in range(-1, 2)], 0), mats[4]).reshape(3, 8, LANES)
    up2_buf[:, pl.ds(0, 8, 2), :] = spread
    up2_buf[:, pl.ds(1, 8, 2), :] = spread

    def lower(tile):
        return jnp.where(low, tile, pltpu.roll(tile, 64, 1))

    def upper(tile):
        return jnp.where(low, pltpu.roll(tile, 64, 1), tile)

    f2 = {
        -2: upper(f2_in[0]) + upper(f2_in[4]),
        -1: share[0] + lower(f2_in[1]),
        0: share[1] + upper(f2_in[1]),
        1: share[2] + lower(f2_in[2]),
        2: share[3] + upper(f2_in[2]),
        3: lower(f2_in[3]) + lower(f2_in[5]),
    }
    fixed = {p: C2 * f2[p] + up2_buf[(p >> 1) + 1] for p in range(-2, 4)}
    value = [
        fixed[p] * THIRD + C2 * f2[p] + K2 * ((fixed[p - 1] + fixed[p + 1]) + beside(fixed[p], 32))
        for p in range(-1, 3)
    ]
    spread = times(jnp.concatenate(value, 0), mats[5]).reshape(4, 16, LANES)
    up1_buf[:, pl.ds(0, 16, 2), :] = spread
    up1_buf[:, pl.ds(1, 16, 2), :] = spread
    fixed = {p: C1 * f1_buf[p + 2] + up1_buf[(p >> 1) + 1] for p in range(-2, 6)}
    error = jnp.concatenate(
        [
            fixed[p] * THIRD + C1 * f1_buf[p + 2]
            + K1 * ((fixed[p - 1] + fixed[p + 1]) + beside(fixed[p], 64))
            for p in range(-1, 5)
        ],
        0,
    )

    for matrix, up_buf, field, shift, last in ((6, uph_buf, h_buf, 1, a_buf), (7, upo_buf, o_buf, 2, b_buf)):
        spread = times(error, mats[matrix]).reshape(6, 32, LANES)
        up_buf[:, pl.ds(0, 32, 2), :] = spread
        up_buf[:, pl.ds(1, 32, 2), :] = spread
        fixed = {}
        for p in range(-1, PLANES + 1):
            fixed[p] = C0 * field[p + shift] + up_buf[(p >> 1) + 1]
            if p >= 1:
                value = fixed[p - 1]
                around = (fixed[p - 2] + fixed[p]) + beside(value)
                last[p - 1] = value * THIRD + C0 * field[p - 1 + shift] + K0 * around
    with jax.named_scope("w_ez"):
        take(ez_sem.at[1], e_z.at[pl.ds(0, RING - 1)])
    sums = jnp.sum(e_z[...], axis=0)
    numer = jnp.sum(jnp.where(lane_row < 64, sums, 0.0), axis=1, keepdims=True)
    denom = jnp.sum(jnp.where(lane_row < 64, 0.0, sums), axis=1, keepdims=True)
    energy = numer / denom

    def finish(p):
        value = a_buf[p] - energy * b_buf[p]
        out_ref[0, p] = value
        return value.astype(jnp.bfloat16)

    for step, other in ((2, False), (2, True), (1, False), (-1, False), (1, True), (-1, True), (0, True)):
        to = state_at(step, other)
        rounded[to] = finish(to)
        send(rounded.at[to], mixed.at[s], (x_sem.at[0], x_sem.at[1]), (g, to))
    mixed[s] = finish(s)
    with jax.named_scope("w_mix"):
        take(x_sem.at[1], mixed.at[pl.ds(0, STATES - 1)])

    pairs = [(i, j) for i in range(STATES) for j in range(i, STATES)]
    held = {pair: None for pair in pairs}
    for block in range(ROWS // 16):
        values = [mixed[i, 16 * block : 16 * block + 16].astype(F32) for i in range(STATES)]
        for i, j in pairs:
            product = values[i] * values[j]
            product = product[:8] + product[8:]
            held[i, j] = product if held[i, j] is None else held[i, j] + product
    for i, j in pairs:
        row = jnp.sum(held[i, j], 0, keepdims=True)
        rows_buf[8 * i + j : 8 * i + j + 1] = row
        if i != j:
            rows_buf[8 * j + i : 8 * j + i + 1] = row
    flat = lax.dot_general(
        jnp.ones((8, LANES), F32), rows_buf[...], (((1,), (1,)), ((), ())),
        precision=HIGH, preferred_element_type=F32,
    )
    g_z[z] = flat[:1]
    for d in range(1, RING):
        send(g_z.at[z], g_z.at[z], (gz_sem.at[0], gz_sem.at[1]), on_ring(d))
    with jax.named_scope("w_gz"):
        take(gz_sem.at[1], g_z.at[pl.ds(0, RING - 1)])
    mine = y * STATES + s
    g_xy[mine] = jnp.sum(g_z[...], axis=0)
    for d in range(1, STATES * columns):
        send(g_xy.at[mine], g_xy.at[mine], (gx_sem.at[0], gx_sem.at[1]), on_face(d))
    with jax.named_scope("w_sends"):
        take(halo_send, o_buf.at[pl.ds(0, 6)])
        take(f1_sem.at[0], f1_buf.at[pl.ds(0, 4)])
        take(f2_sem.at[0], f2_in)
        take(f3_sem.at[0], f3_in.at[pl.ds(0, 2 * REACH)])
        take(ey_sem.at[0], e_y.at[pl.ds(0, columns - 1)])
        take(ez_sem.at[0], e_z.at[pl.ds(0, RING - 1)])
        take(x_sem.at[0], mixed.at[pl.ds(0, STATES - 1)])
        take(gz_sem.at[0], g_z.at[pl.ds(0, RING - 1)])
    with jax.named_scope("w_gxy"):
        take(gx_sem.at[1], g_xy.at[pl.ds(0, STATES * columns - 1)])
    total = jnp.sum(g_xy[...], axis=0)
    picked = jnp.zeros((1, STATES), F32)
    for t in range(STATES):
        picked += jnp.where(s == t, total[:, STATES * t : STATES * t + STATES], 0.0)
    gram_ref[...] = picked / F32(PLANES * ROWS * LANES * slabs)
    with jax.named_scope("w_last"):
        take(gx_sem.at[0], g_xy.at[pl.ds(0, STATES * columns - 1)])


def solution(mesh):
    slabs = mesh.shape["grid"]
    columns = slabs // RING
    faces = STATES * columns
    dma = pltpu.SemaphoreType.DMA

    def vmem(*shape, dtype=F32):
        return pltpu.VMEM(shape, dtype)

    def on_device(orbitals, potential):
        return pl.pallas_call(
            functools.partial(kernel, slabs),
            out_shape=(
                jax.ShapeDtypeStruct((1, PLANES, ROWS, LANES), F32),
                jax.ShapeDtypeStruct((1, STATES), F32),
            ),
            in_specs=[pl.BlockSpec(memory_space=pltpu.HBM)] * 2,
            out_specs=(
                pl.BlockSpec(memory_space=pltpu.VMEM),
                pl.BlockSpec(memory_space=pltpu.VMEM),
            ),
            scratch_shapes=[
                vmem(PLANES + 4, ROWS, LANES),
                vmem(PLANES, ROWS, LANES),
                vmem(PLANES + 2, ROWS, LANES),
                vmem(PLANES, ROWS, LANES),
                vmem(2, ROWS, LANES),
                vmem(2, ROWS, LANES),
                vmem(PLANES, ROWS, LANES),
                vmem(8, LANES, LANES),
                vmem(8, 32, LANES),
                vmem(4, 32, LANES),
                vmem(2, 16, LANES),
                vmem(6, 16, LANES),
                vmem(3, 16, LANES),
                vmem(2 * REACH + 1, 8, LANES),
                vmem(3, 16, LANES),
                vmem(4, 32, LANES),
                vmem(6, ROWS, LANES),
                vmem(6, ROWS, LANES),
                vmem(PLANES, ROWS, LANES),
                vmem(PLANES, ROWS, LANES),
                vmem(columns, 1, LANES),
                vmem(RING, 1, LANES),
                vmem(PLANES, ROWS, LANES, dtype=jnp.bfloat16),
                vmem(STATES, ROWS, LANES, dtype=jnp.bfloat16),
                vmem(LANES, LANES),
                vmem(RING, 1, LANES),
                vmem(faces, 1, LANES),
                dma((2,)), dma(()), dma((3,)), dma((2,)), dma((2,)), dma((2,)),
                dma((2,)), dma((2,)), dma((2,)), dma((2,)), dma((2,)),
                pltpu.SemaphoreType.REGULAR((3,)),
            ],
            compiler_params=pltpu.CompilerParams(
                collective_id=0, has_side_effects=True, vmem_limit_bytes=32 * 1024 * 1024
            ),
        )(*[pltpu.with_memory_space_constraint(v, pltpu.HBM) for v in (orbitals, potential)])

    return jax.shard_map(
        on_device,
        mesh=mesh,
        in_specs=(P("state", "grid", None, None), P("grid", None, None)),
        out_specs=(P("state", "grid", None, None), P("state", None)),
        check_vma=False,
    )
```

time: 55.2 us -> 48.1 us (0.87)
  Pallas kernels: 51.3 us -> 46.1 us
  local copies, waits for them, and re-layouts: 3.11 us -> 1.22 us
    pallas_call x1, Pallas kernels: 51.3 us -> 46.1 us  [on_device(): pl.pallas_call(functools.partial(kernel, slabs), out_shape=(jax.ShapeDtyp...]
    unnamed x6 -> x2, local copies, waits for them, and re-layouts: 3.11 us -> 1.22 us
where the time goes in v2:
time: 48.1 us; the launch traced here: 48 us
  Pallas kernels  46.1 us (96%)
  local copies, waits for them, and re-layouts  1.22 us (3%)
  between operations  0.64 us (1%)
    pallas_call x1, Pallas kernels, on_device(): pl.pallas_call(functools.partial(kernel, slabs), out_shape=(jax.ShapeDtyp...  46.1 us
    unnamed x2, local copies, waits for them, and re-layouts  1.22 us

profile of v2, /device:TPU:1, one launch (start us, length us, event | category | flops | bytes accessed | tf_op | source)
XLA Modules:
  0.0 48.0 jit_solution(14796057326041994609)
XLA Ops:
  0.6 46.1 %shard_map.41 = (f32[1,8,64,128]{3,2,1,0:T(8,128)S(1)}, f32[1,8]{1,0:T(1,128)S(1)}) custom-call(f32[1,8,64,128]{3,2,1,0:T(8,128)} %o_hbm.1, f32[8,64,128]{2,1,0:T(8,128)} %p_hbm.1), custom_call_target="tpu_custom_call" | custom-call | tf_op jit(solution)/shard_map/pallas_call | solution.py:421
  46.8 0.7 %copy.6 = f32[1,8,64,128]{3,2,1,0:T(8,128)} copy(f32[1,8,64,128]{3,2,1,0:T(8,128)S(1)} %get-tuple-element.4) | data formatting | bytes 524288
  47.5 0.5 %copy.7 = f32[1,8]{1,0:T(1,128)} copy(f32[1,8]{1,0:T(1,128)S(1)} %get-tuple-element.5) | data formatting | bytes 64

commit v3 on v2

--- a/solution.py
+++ b/solution.py
@@ -92,25 +92,25 @@
     token,
 ):
     g, s = lax.axis_index("grid"), lax.axis_index("state")
-    y, z = g // RING, g % RING
-    x, core = s // 2, s % 2
+    y, z = g >> 4, g & (RING - 1)
+    x, core = s >> 1, s & 1
     columns = slabs // RING
 
     def slab(step):
-        return (lax.rem(g + step + slabs, slabs), s)
+        return ((g + step) & (slabs - 1), s)
 
     def on_ring(step):
-        return (y * RING + lax.rem(z + step + RING, RING), s)
+        return (y * RING + ((z + step) & (RING - 1)), s)
 
     def on_column(step):
-        return (lax.rem(y + step + columns, columns) * RING + z, s)
+        return (((y + step) & (columns - 1)) * RING + z, s)
 
     def state_at(step, other):
-        return 2 * lax.rem(x + step + CHIPS, CHIPS) + (lax.rem(core + 1, 2) if other else core)
+        return 2 * ((x + step) & (CHIPS - 1)) + (1 - core if other else core)
 
     def on_face(step):
         up, side = step // STATES, step % STATES
-        return (lax.rem(y + up, columns) * RING + z, lax.rem(s + side, STATES))
+        return (((y + up) & (columns - 1)) * RING + z, (s + side) & (STATES - 1))
 
     def send(src, dst, sems, peer):
         copy = pltpu.make_async_remote_copy(
@@ -126,11 +126,12 @@
         for peer in peers:
             pl.semaphore_signal(sem, inc=1, device_id=peer, device_id_type=MESH)
 
-    partner = (g, state_at(0, True))
-    close = [slab(1), slab(-1), on_ring(1), on_ring(-1), on_column(1), on_column(-1)]
-    close += [(g, state_at(1, False)), (g, state_at(-1, False))]
+    others = [(step, other) for step in (2, 1, -1) for other in (False, True)] + [(0, True)]
+    next_two = [slab(1), slab(-1), on_ring(2), on_ring(-2)]
+    close = next_two + [on_column(2)] + [(g, state_at(*pair)) for pair in others]
+    close += [on_ring(1), on_ring(-1), on_column(1), on_column(-1)]
     barrier = pltpu.get_barrier_semaphore()
-    signal(barrier, close + [partner])
+    signal(barrier, close)
     loads = [
         pltpu.make_async_copy(o_hbm.at[0], o_buf.at[pl.ds(2, PLANES)], load_sem.at[0]),
         pltpu.make_async_copy(p_hbm, p_buf, load_sem.at[1]),
@@ -138,7 +139,7 @@
     for load in loads:
         load.start()
     with jax.named_scope("w_barrier"):
-        pl.semaphore_wait(barrier, len(close) + 1)
+        pl.semaphore_wait(barrier, len(close))
 
     right, left = slab(1), slab(-1)
 
@@ -147,20 +148,13 @@
         send(o_hbm.at[0, pl.ds(6, 2), pl.ds(mine, HALF)], o_buf.at[pl.ds(0, 2), pl.ds(mine, HALF)], sems, right)
         send(o_hbm.at[0, pl.ds(0, 2), pl.ds(theirs, HALF)], o_buf.at[pl.ds(10, 2), pl.ds(theirs, HALF)], sems, left)
 
-    signal(token.at[0], close)
+    signal(token.at[0], next_two)
     halo(0, 0, HALF)
     with jax.named_scope("w_load"):
         for load in loads:
             load.wait()
     g_out[0] = p_buf[0] * o_buf[2] + FAR * o_buf[4]
     g_out[1] = p_buf[7] * o_buf[9] + FAR * o_buf[7]
-    with jax.named_scope("w_t1"):
-        pl.semaphore_wait(token.at[0], len(close))
-    signal(token.at[1], [slab(2), slab(-2), on_ring(2), on_ring(-2)])
-    halo(1, HALF, 0)
-    sems = (halo_send, halo_recv.at[2])
-    send(g_out.at[1], g_in.at[0], sems, right)
-    send(g_out.at[0], g_in.at[1], sems, left)
 
     top = jnp.zeros((ROWS, LANES), F32)
     bottom = jnp.zeros((ROWS, LANES), F32)
@@ -178,15 +172,20 @@
         r_buf[p] = centre * THIRD + K0 * first
         top += centre * value
         bottom += centre * centre
+    halo(1, HALF, 0)
+    sems = (halo_send, halo_recv.at[2])
+    send(g_out.at[1], g_in.at[0], sems, right)
+    send(g_out.at[0], g_in.at[1], sems, left)
     for index, matrix in enumerate(matrices()):
         mats[index] = matrix
     rows_buf[...] = jnp.zeros_like(rows_buf)
     top, bottom = jnp.sum(top, 0, keepdims=True), jnp.sum(bottom, 0, keepdims=True)
     lane_row = iota((1, LANES), 1)
-    with jax.named_scope("w_t2"):
-        pl.semaphore_wait(token.at[1], 4)
-    signal(token.at[2], [on_ring(4), on_ring(-4), partner])
-
+
+    with jax.named_scope("w_t1"):
+        pl.semaphore_wait(token.at[0], len(next_two))
+    signal(token.at[1], [on_ring(4), on_ring(-4)])
+    signal(token.at[2], [slab(2), slab(-2)])
     with jax.named_scope("w_halo_a"):
         take(halo_recv.at[0], o_buf.at[pl.ds(0, 2)])
     cross = o_buf[2, :HALF] * (2.0 * NEAR * o_buf[1, :HALF] + 2.0 * FAR * o_buf[0, :HALF])
@@ -228,6 +227,9 @@
     )
     f1 = f1.reshape(4, 32, LANES)
     f1_buf[2:6] = f1
+    sems = (f1_sem.at[0], f1_sem.at[1])
+    send(f1_buf.at[pl.ds(4, 2)], f1_buf.at[pl.ds(0, 2)], sems, right)
+    send(f1_buf.at[pl.ds(2, 2)], f1_buf.at[pl.ds(6, 2)], sems, left)
 
     rest = []
     for p in range(4):
@@ -242,9 +244,9 @@
     two_buf[3] = K1 * f1[3]
     halved = two_buf[:, pl.ds(0, 16, 2), :] + two_buf[:, pl.ds(1, 16, 2), :]
     share = times(halved.reshape(64, LANES), mats[2]).reshape(4, 16, LANES)
-    low = iota((16, LANES), 1) < 64
-    f2_out[0] = jnp.where(low, share[0], share[1])
-    f2_out[1] = jnp.where(low, share[2], share[3])
+    low = iota((8, LANES), 1) < 64
+    for k in range(4):
+        f2_out[k] = jnp.where(low, share[k][:8], share[k][8:])
     a, b, c, d = share[0], share[1], share[2], share[3]
     three_buf[0] = a * (K2 + THIRD) + K2 * (b + beside(a, 32))
     three_buf[1] = (b + c) * (THIRD + K2) + K2 * ((a + d) + (beside(b, 32) + beside(c, 32)))
@@ -256,26 +258,25 @@
         lane < 32, parts[0],
         jnp.where(lane < 64, parts[1], jnp.where(lane < 96, parts[2], 0.0)),
     )
+    with jax.named_scope("w_t2"):
+        pl.semaphore_wait(token.at[2], 2)
     sems = (f3_sem.at[0], f3_sem.at[1])
     for step in range(REACH, 0, -1):
         send(f3_in.at[REACH], f3_in.at[REACH - step], sems, slab(step))
         send(f3_in.at[REACH], f3_in.at[REACH + step], sems, slab(-step))
+    sems = (f2_sem.at[0], f2_sem.at[1])
+    send(f2_out.at[pl.ds(1, 3)], f2_in.at[pl.ds(0, 3)], sems, right)
+    send(f2_out.at[pl.ds(0, 3)], f2_in.at[pl.ds(3, 3)], sems, left)
+    send(f2_out.at[3], f2_in.at[6], sems, slab(2))
+    send(f2_out.at[0], f2_in.at[7], sems, slab(-2))
 
     with jax.named_scope("w_ey"):
         take(ey_sem.at[1], e_y.at[pl.ds(0, columns - 1)])
     e_z[z] = jnp.sum(e_y[...], axis=0)
     with jax.named_scope("w_t3"):
-        pl.semaphore_wait(token.at[2], 3)
+        pl.semaphore_wait(token.at[1], 2)
     for d in range(1, RING):
         send(e_z.at[z], e_z.at[z], (ez_sem.at[0], ez_sem.at[1]), on_ring(d))
-    sems = (f2_sem.at[0], f2_sem.at[1])
-    send(f2_out, f2_in.at[pl.ds(0, 2)], sems, right)
-    send(f2_out, f2_in.at[pl.ds(2, 2)], sems, left)
-    send(f2_out.at[1], f2_in.at[4], sems, slab(2))
-    send(f2_out.at[0], f2_in.at[5], sems, slab(-2))
-    sems = (f1_sem.at[0], f1_sem.at[1])
-    send(f1_buf.at[pl.ds(4, 2)], f1_buf.at[pl.ds(0, 2)], sems, right)
-    send(f1_buf.at[pl.ds(2, 2)], f1_buf.at[pl.ds(6, 2)], sems, left)
 
     with jax.named_scope("w_f"):
         take(f3_sem.at[1], f3_in.at[pl.ds(0, 2 * REACH)])
@@ -299,19 +300,17 @@
     up2_buf[:, pl.ds(0, 8, 2), :] = spread
     up2_buf[:, pl.ds(1, 8, 2), :] = spread
 
-    def lower(tile):
-        return jnp.where(low, tile, pltpu.roll(tile, 64, 1))
-
-    def upper(tile):
-        return jnp.where(low, pltpu.roll(tile, 64, 1), tile)
+    def unfold(tile):
+        turned = pltpu.roll(tile, 64, 1)
+        return jnp.concatenate([jnp.where(low, tile, turned), jnp.where(low, turned, tile)], 0)
 
     f2 = {
-        -2: upper(f2_in[0]) + upper(f2_in[4]),
-        -1: share[0] + lower(f2_in[1]),
-        0: share[1] + upper(f2_in[1]),
-        1: share[2] + lower(f2_in[2]),
-        2: share[3] + upper(f2_in[2]),
-        3: lower(f2_in[3]) + lower(f2_in[5]),
+        -2: unfold(f2_in[0] + f2_in[6]),
+        -1: share[0] + unfold(f2_in[1]),
+        0: share[1] + unfold(f2_in[2]),
+        1: share[2] + unfold(f2_in[3]),
+        2: share[3] + unfold(f2_in[4]),
+        3: unfold(f2_in[5] + f2_in[7]),
     }
     fixed = {p: C2 * f2[p] + up2_buf[(p >> 1) + 1] for p in range(-2, 4)}
     value = [
@@ -354,7 +353,7 @@
         out_ref[0, p] = value
         return value.astype(jnp.bfloat16)
 
-    for step, other in ((2, False), (2, True), (1, False), (-1, False), (1, True), (-1, True), (0, True)):
+    for step, other in others:
         to = state_at(step, other)
         rounded[to] = finish(to)
         send(rounded.at[to], mixed.at[s], (x_sem.at[0], x_sem.at[1]), (g, to))
@@ -417,8 +416,22 @@
     def vmem(*shape, dtype=F32):
         return pltpu.VMEM(shape, dtype)
 
+    def write_out(values, gram, values_hbm, gram_hbm, sem):
+        copies = [
+            pltpu.make_async_copy(values, values_hbm, sem.at[0]),
+            pltpu.make_async_copy(gram, gram_hbm, sem.at[1]),
+        ]
+        for copy in copies:
+            copy.start()
+        for copy in copies:
+            copy.wait()
+
     def on_device(orbitals, potential):
-        return pl.pallas_call(
+        shapes = (
+            jax.ShapeDtypeStruct((1, PLANES, ROWS, LANES), F32),
+            jax.ShapeDtypeStruct((1, STATES), F32),
+        )
+        results = pl.pallas_call(
             functools.partial(kernel, slabs),
             out_shape=(
                 jax.ShapeDtypeStruct((1, PLANES, ROWS, LANES), F32),
@@ -440,8 +453,8 @@
                 vmem(8, LANES, LANES),
                 vmem(8, 32, LANES),
                 vmem(4, 32, LANES),
-                vmem(2, 16, LANES),
-                vmem(6, 16, LANES),
+                vmem(4, 8, LANES),
+                vmem(8, 8, LANES),
                 vmem(3, 16, LANES),
                 vmem(2 * REACH + 1, 8, LANES),
                 vmem(3, 16, LANES),
@@ -466,6 +479,15 @@
             ),
         )(*[pltpu.with_memory_space_constraint(v, pltpu.HBM) for v in (orbitals, potential)])
 
+        return pl.pallas_call(
+            write_out,
+            out_shape=shapes,
+            in_specs=[pl.BlockSpec(memory_space=pltpu.VMEM)] * 2,
+            out_specs=(pl.BlockSpec(memory_space=pltpu.HBM), pl.BlockSpec(memory_space=pltpu.HBM)),
+            scratch_shapes=[dma((2,))],
+            compiler_params=pltpu.CompilerParams(vmem_limit_bytes=1024 * 1024),
+        )(*results)
+
     return jax.shard_map(
         on_device,
         mesh=mesh,

time: 48.1 us -> 46.8 us (0.973)
  local copies, waits for them, and re-layouts: 1.22 us -> 0 us
    unnamed x2 -> x0, local copies, waits for them, and re-layouts: 1.22 us -> none
    pallas_call x1, Pallas kernels: 46.1 us -> 45.3 us  [on_device(): pl.pallas_call(functools.partial(kernel, slabs), out_shape=(jax.ShapeDtyp...]
    pallas_call x0 -> x1, Pallas kernels: none -> 0.72 us  [on_device(): pl.pallas_call(write_out, out_shape=shapes, in_specs=[pl.BlockSpec(memory...]
where the time goes in v3:
time: 46.8 us; the launch traced here: 46.7 us
  Pallas kernels  46 us (98%)
  between operations  0.64 us (1%)
    pallas_call x1, Pallas kernels, on_device(): pl.pallas_call(functools.partial(kernel, slabs), out_shape=(jax.ShapeDtyp...  45.3 us

profile of v3, /device:TPU:1, one launch (start us, length us, event | category | flops | bytes accessed | tf_op | source)
XLA Modules:
  0.0 46.7 jit_solution(7889983565410969180)
XLA Ops:
  0.6 45.3 %shard_map.41 = (f32[1,8,64,128]{3,2,1,0:T(8,128)S(1)}, f32[1,8]{1,0:T(1,128)S(1)}) custom-call(f32[1,8,64,128]{3,2,1,0:T(8,128)} %o_hbm.1, f32[8,64,128]{2,1,0:T(8,128)} %p_hbm.1), custom_call_target="tpu_custom_call" | custom-call | tf_op jit(solution)/shard_map/pallas_call | solution.py:434
  46.0 0.7 %shard_map.42 = (f32[1,8,64,128]{3,2,1,0:T(8,128)}, f32[1,8]{1,0:T(1,128)}) custom-call(f32[1,8,64,128]{3,2,1,0:T(8,128)S(1)} %get-tuple-element.4.values, f32[1,8]{1,0:T(1,128)S(1)} %get-tuple-element.5.gram), custom_call_target="tpu_custom_call" | custom-call | tf_op jit(solution)/shard_map/pallas_call | solution.py:482

commit v4 on v3

--- a/solution.py
+++ b/solution.py
@@ -87,7 +87,7 @@
     o_buf, p_buf, h_buf, r_buf, g_out, g_in, pair_buf, mats,
     f1_buf, two_buf, f2_out, f2_in, three_buf, f3_in,
     up2_buf, up1_buf, uph_buf, upo_buf, a_buf, b_buf,
-    e_y, e_z, rounded, mixed, rows_buf, g_z, g_xy,
+    e_y, e_z, rounded, mixed, rows_buf, g_z, g_xy, wide,
     load_sem, halo_send, halo_recv, f1_sem, f2_sem, f3_sem, ey_sem, ez_sem, x_sem, gz_sem, gx_sem,
     token,
 ):
@@ -128,8 +128,9 @@
 
     others = [(step, other) for step in (2, 1, -1) for other in (False, True)] + [(0, True)]
     next_two = [slab(1), slab(-1), on_ring(2), on_ring(-2)]
-    close = next_two + [on_column(2)] + [(g, state_at(*pair)) for pair in others]
-    close += [on_ring(1), on_ring(-1), on_column(1), on_column(-1)]
+    partner = (g, state_at(0, True))
+    next_two += [on_column(1), on_column(-1), (g, state_at(1, False)), (g, state_at(-1, False))]
+    close = next_two + [on_ring(1), on_ring(-1), partner]
     barrier = pltpu.get_barrier_semaphore()
     signal(barrier, close)
     loads = [
@@ -138,21 +139,21 @@
     ]
     for load in loads:
         load.start()
-    with jax.named_scope("w_barrier"):
-        pl.semaphore_wait(barrier, len(close))
-
-    right, left = slab(1), slab(-1)
-
-    def halo(part, mine, theirs):
-        sems = (halo_send, halo_recv.at[part])
-        send(o_hbm.at[0, pl.ds(6, 2), pl.ds(mine, HALF)], o_buf.at[pl.ds(0, 2), pl.ds(mine, HALF)], sems, right)
-        send(o_hbm.at[0, pl.ds(0, 2), pl.ds(theirs, HALF)], o_buf.at[pl.ds(10, 2), pl.ds(theirs, HALF)], sems, left)
-
-    signal(token.at[0], next_two)
-    halo(0, 0, HALF)
     with jax.named_scope("w_load"):
         for load in loads:
             load.wait()
+    with jax.named_scope("w_barrier"):
+        pl.semaphore_wait(barrier, len(close))
+
+    right, left = slab(1), slab(-1)
+
+    def halo(part, mine, theirs):
+        sems = (halo_send, halo_recv.at[part])
+        send(o_buf.at[pl.ds(8, 2), pl.ds(mine, HALF)], o_buf.at[pl.ds(0, 2), pl.ds(mine, HALF)], sems, right)
+        send(o_buf.at[pl.ds(2, 2), pl.ds(theirs, HALF)], o_buf.at[pl.ds(10, 2), pl.ds(theirs, HALF)], sems, left)
+
+    signal(token.at[0], next_two)
+    halo(0, 0, HALF)
     g_out[0] = p_buf[0] * o_buf[2] + FAR * o_buf[4]
     g_out[1] = p_buf[7] * o_buf[9] + FAR * o_buf[7]
 
@@ -176,15 +177,18 @@
     sems = (halo_send, halo_recv.at[2])
     send(g_out.at[1], g_in.at[0], sems, right)
     send(g_out.at[0], g_in.at[1], sems, left)
-    for index, matrix in enumerate(matrices()):
-        mats[index] = matrix
+    made = matrices()
+    for index in range(6):
+        mats[index] = made[index]
+    wide[:, :LANES] = made[6]
+    wide[:, LANES:] = made[7]
     rows_buf[...] = jnp.zeros_like(rows_buf)
     top, bottom = jnp.sum(top, 0, keepdims=True), jnp.sum(bottom, 0, keepdims=True)
     lane_row = iota((1, LANES), 1)
 
     with jax.named_scope("w_t1"):
         pl.semaphore_wait(token.at[0], len(next_two))
-    signal(token.at[1], [on_ring(4), on_ring(-4)])
+    signal(token.at[1], [on_ring(4), on_ring(-4), partner])
     signal(token.at[2], [slab(2), slab(-2)])
     with jax.named_scope("w_halo_a"):
         take(halo_recv.at[0], o_buf.at[pl.ds(0, 2)])
@@ -196,7 +200,7 @@
     e_y[y] = jnp.where(
         lane_row < 64, top + pltpu.roll(top, 64, 1), bottom + pltpu.roll(bottom, 64, 1)
     )
-    for d in range(1, columns):
+    for d in (2, 1, 3):
         send(e_y.at[y], e_y.at[y], (ey_sem.at[0], ey_sem.at[1]), on_column(d))
 
     with jax.named_scope("w_halo_b"):
@@ -218,13 +222,14 @@
         for p in (2 * q, 2 * q + 1):
             value = h_buf[p + 1]
             rest = value * THIRD + K0 * ((h_buf[p] + h_buf[p + 2]) + beside(value))
+            a_buf[p] = C0 * (value + rest)
+            b_buf[p] = C0 * (o_buf[p + 2] + r_buf[p])
             both = rest if both is None else both + rest
         pair_buf[q] = both
         pair_buf[q + 4] = r_buf[2 * q] + r_buf[2 * q + 1]
     halved = pair_buf[:, pl.ds(0, 32, 2), :] + pair_buf[:, pl.ds(1, 32, 2), :]
-    f1 = times(halved[:4].reshape(LANES, LANES), mats[0]) + times(
-        halved[4:].reshape(LANES, LANES), mats[1]
-    )
+    halved = [halved[:4].reshape(LANES, LANES), halved[4:].reshape(LANES, LANES)]
+    f1 = times(jnp.concatenate(halved, 1), mats[0:2].reshape(2 * LANES, LANES))
     f1 = f1.reshape(4, 32, LANES)
     f1_buf[2:6] = f1
     sems = (f1_sem.at[0], f1_sem.at[1])
@@ -274,8 +279,8 @@
         take(ey_sem.at[1], e_y.at[pl.ds(0, columns - 1)])
     e_z[z] = jnp.sum(e_y[...], axis=0)
     with jax.named_scope("w_t3"):
-        pl.semaphore_wait(token.at[1], 2)
-    for d in range(1, RING):
+        pl.semaphore_wait(token.at[1], 3)
+    for d in sorted(range(1, RING), key=lambda d: abs(d - RING // 2)):
         send(e_z.at[z], e_z.at[z], (ez_sem.at[0], ez_sem.at[1]), on_ring(d))
 
     with jax.named_scope("w_f"):
@@ -330,17 +335,16 @@
         0,
     )
 
-    for matrix, up_buf, field, shift, last in ((6, uph_buf, h_buf, 1, a_buf), (7, upo_buf, o_buf, 2, b_buf)):
-        spread = times(error, mats[matrix]).reshape(6, 32, LANES)
-        up_buf[:, pl.ds(0, 32, 2), :] = spread
-        up_buf[:, pl.ds(1, 32, 2), :] = spread
-        fixed = {}
-        for p in range(-1, PLANES + 1):
-            fixed[p] = C0 * field[p + shift] + up_buf[(p >> 1) + 1]
-            if p >= 1:
-                value = fixed[p - 1]
-                around = (fixed[p - 2] + fixed[p]) + beside(value)
-                last[p - 1] = value * THIRD + C0 * field[p - 1 + shift] + K0 * around
+    spread = times(error, wide[...])
+    for at, up_buf, last in ((0, uph_buf, a_buf), (LANES, upo_buf, b_buf)):
+        part = spread[:, at : at + LANES].reshape(6, 32, LANES)
+        up_buf[:, pl.ds(0, 32, 2), :] = part
+        up_buf[:, pl.ds(1, 32, 2), :] = part
+        for q in range(1, 5):
+            value = up_buf[q]
+            same = value * (THIRD + K0) + K0 * beside(value)
+            last[2 * q - 2] += same + K0 * up_buf[q - 1]
+            last[2 * q - 1] += same + K0 * up_buf[q + 1]
     with jax.named_scope("w_ez"):
         take(ez_sem.at[1], e_z.at[pl.ds(0, RING - 1)])
     sums = jnp.sum(e_z[...], axis=0)
@@ -379,13 +383,13 @@
         precision=HIGH, preferred_element_type=F32,
     )
     g_z[z] = flat[:1]
-    for d in range(1, RING):
+    for d in sorted(range(1, RING), key=lambda d: abs(d - RING // 2)):
         send(g_z.at[z], g_z.at[z], (gz_sem.at[0], gz_sem.at[1]), on_ring(d))
     with jax.named_scope("w_gz"):
         take(gz_sem.at[1], g_z.at[pl.ds(0, RING - 1)])
     mine = y * STATES + s
     g_xy[mine] = jnp.sum(g_z[...], axis=0)
-    for d in range(1, STATES * columns):
+    for d in sorted(range(1, STATES * columns), key=lambda d: abs(d // STATES - 2) + abs(d % STATES - 4) / 2):
         send(g_xy.at[mine], g_xy.at[mine], (gx_sem.at[0], gx_sem.at[1]), on_face(d))
     with jax.named_scope("w_sends"):
         take(halo_send, o_buf.at[pl.ds(0, 6)])
@@ -450,7 +454,7 @@
                 vmem(2, ROWS, LANES),
                 vmem(2, ROWS, LANES),
                 vmem(PLANES, ROWS, LANES),
-                vmem(8, LANES, LANES),
+                vmem(6, LANES, LANES),
                 vmem(8, 32, LANES),
                 vmem(4, 32, LANES),
                 vmem(4, 8, LANES),
@@ -470,6 +474,7 @@
                 vmem(LANES, LANES),
                 vmem(RING, 1, LANES),
                 vmem(faces, 1, LANES),
+                vmem(LANES, 2 * LANES),
                 dma((2,)), dma(()), dma((3,)), dma((2,)), dma((2,)), dma((2,)),
                 dma((2,)), dma((2,)), dma((2,)), dma((2,)), dma((2,)),
                 pltpu.SemaphoreType.REGULAR((3,)),

time: 46.8 us -> 45.8 us (0.979)
  Pallas kernels: 46 us -> 45 us
    pallas_call x1, Pallas kernels: 45.3 us -> 44.3 us  [on_device(): pl.pallas_call(functools.partial(kernel, slabs), out_shape=(jax.ShapeDtyp...]
where the time goes in v4:
time: 45.8 us; the launch traced here: 45.7 us
  Pallas kernels  45 us (98%)
  between operations  0.64 us (1%)
    pallas_call x1, Pallas kernels, on_device(): pl.pallas_call(functools.partial(kernel, slabs), out_shape=(jax.ShapeDtyp...  44.3 us

profile of v4, /device:TPU:1, one launch (start us, length us, event | category | flops | bytes accessed | tf_op | source)
XLA Modules:
  0.0 45.7 jit_solution(1289910062822077384)
XLA Ops:
  0.6 44.3 %shard_map.41 = (f32[1,8,64,128]{3,2,1,0:T(8,128)S(1)}, f32[1,8]{1,0:T(1,128)S(1)}) custom-call(f32[1,8,64,128]{3,2,1,0:T(8,128)} %o_hbm.1, f32[8,64,128]{2,1,0:T(8,128)} %p_hbm.1), custom_call_target="tpu_custom_call" | custom-call | tf_op jit(solution)/shard_map/pallas_call | solution.py:438
  44.9 0.7 %shard_map.42 = (f32[1,8,64,128]{3,2,1,0:T(8,128)}, f32[1,8]{1,0:T(1,128)}) custom-call(f32[1,8,64,128]{3,2,1,0:T(8,128)S(1)} %get-tuple-element.4.values, f32[1,8]{1,0:T(1,128)S(1)} %get-tuple-element.5.gram), custom_call_target="tpu_custom_call" | custom-call | tf_op jit(solution)/shard_map/pallas_call | solution.py:487

commit v5 on v4

--- a/solution.py
+++ b/solution.py
@@ -105,12 +105,19 @@
     def on_column(step):
         return (((y + step) & (columns - 1)) * RING + z, s)
 
+    hub = core == 1
+    chip_states = (s - core, s - core + 1)
+
     def state_at(step, other):
         return 2 * ((x + step) & (CHIPS - 1)) + (1 - core if other else core)
 
     def on_face(step):
         up, side = step // STATES, step % STATES
         return (((y + up) & (columns - 1)) * RING + z, (s + side) & (STATES - 1))
+
+    def each_core(zero, one):
+        pl.when(core == 0)(zero)
+        pl.when(core == 1)(one)
 
     def send(src, dst, sems, peer):
         copy = pltpu.make_async_remote_copy(
@@ -188,7 +195,8 @@
 
     with jax.named_scope("w_t1"):
         pl.semaphore_wait(token.at[0], len(next_two))
-    signal(token.at[1], [on_ring(4), on_ring(-4), partner])
+    signal(token.at[1], [on_ring(4), on_ring(-4)])
+    signal(token.at[3], [partner])
     signal(token.at[2], [slab(2), slab(-2)])
     with jax.named_scope("w_halo_a"):
         take(halo_recv.at[0], o_buf.at[pl.ds(0, 2)])
@@ -197,11 +205,17 @@
     cross += o_buf[9, HALF:] * (2.0 * NEAR * o_buf[10, HALF:] + 2.0 * FAR * o_buf[11, HALF:])
     cross += 2.0 * FAR * o_buf[10, HALF:] * o_buf[8, HALF:]
     top += jnp.sum(cross, 0, keepdims=True)
-    e_y[y] = jnp.where(
+    e_y[core * columns + y] = jnp.where(
         lane_row < 64, top + pltpu.roll(top, 64, 1), bottom + pltpu.roll(bottom, 64, 1)
     )
-    for d in (2, 1, 3):
-        send(e_y.at[y], e_y.at[y], (ey_sem.at[0], ey_sem.at[1]), on_column(d))
+    pl.semaphore_wait(token.at[3], 1)
+
+    def to_hubs(steps):
+        mine = e_y.at[core * columns + y]
+        for d in steps:
+            send(mine, mine, (ey_sem.at[0], ey_sem.at[1]), (on_column(d)[0], chip_states[1]))
+
+    each_core(lambda: to_hubs((2, 1, 3, 0)), lambda: to_hubs((2, 1, 3)))
 
     with jax.named_scope("w_halo_b"):
         take(halo_recv.at[1], o_buf.at[pl.ds(0, 2)])
@@ -275,13 +289,30 @@
     send(f2_out.at[3], f2_in.at[6], sems, slab(2))
     send(f2_out.at[0], f2_in.at[7], sems, slab(-2))
 
-    with jax.named_scope("w_ey"):
-        take(ey_sem.at[1], e_y.at[pl.ds(0, columns - 1)])
-    e_z[z] = jnp.sum(e_y[...], axis=0)
     with jax.named_scope("w_t3"):
-        pl.semaphore_wait(token.at[1], 3)
-    for d in sorted(range(1, RING), key=lambda d: abs(d - RING // 2)):
-        send(e_z.at[z], e_z.at[z], (ez_sem.at[0], ez_sem.at[1]), on_ring(d))
+        pl.semaphore_wait(token.at[1], 2)
+    far_first = sorted(range(1, RING), key=lambda d: abs(d - RING // 2))
+
+    @pl.when(core == 0)
+    def _():
+        signal(token.at[4], [partner])
+
+    @pl.when(hub)
+    def _():
+        pl.semaphore_wait(token.at[4], 1)
+        take(ey_sem.at[1], e_y.at[pl.ds(0, 2 * columns - 1)])
+        first = jnp.sum(e_y[:columns], axis=0)
+        second = jnp.sum(e_y[columns:], axis=0)
+        first, second = first + pltpu.roll(first, 96, 1), second + pltpu.roll(second, 96, 1)
+        e_z[z] = jnp.where(
+            lane_row < 64,
+            jnp.where(lane_row < 32, first, pltpu.roll(first, 96, 1)),
+            jnp.where(lane_row < 96, pltpu.roll(second, 64, 1), pltpu.roll(second, 32, 1)),
+        )
+        for d in far_first:
+            for state in chip_states:
+                send(e_z.at[z], e_z.at[z], (ez_sem.at[0], ez_sem.at[1]), (on_ring(d)[0], state))
+        send(e_z.at[z], e_z.at[z], (ez_sem.at[0], ez_sem.at[1]), partner)
 
     with jax.named_scope("w_f"):
         take(f3_sem.at[1], f3_in.at[pl.ds(0, 2 * REACH)])
@@ -345,11 +376,15 @@
             same = value * (THIRD + K0) + K0 * beside(value)
             last[2 * q - 2] += same + K0 * up_buf[q - 1]
             last[2 * q - 1] += same + K0 * up_buf[q + 1]
+    each_core(
+        lambda: take(ez_sem.at[1], e_z.at[pl.ds(0, RING)]),
+        lambda: take(ez_sem.at[1], e_z.at[pl.ds(0, RING - 1)]),
+    )
     with jax.named_scope("w_ez"):
-        take(ez_sem.at[1], e_z.at[pl.ds(0, RING - 1)])
-    sums = jnp.sum(e_z[...], axis=0)
-    numer = jnp.sum(jnp.where(lane_row < 64, sums, 0.0), axis=1, keepdims=True)
-    denom = jnp.sum(jnp.where(lane_row < 64, 0.0, sums), axis=1, keepdims=True)
+        sums = jnp.sum(e_z[...], axis=0)
+    part = lane_row >> 5
+    numer = jnp.sum(jnp.where(part == 2 * core, sums, 0.0), axis=1, keepdims=True)
+    denom = jnp.sum(jnp.where(part == 2 * core + 1, sums, 0.0), axis=1, keepdims=True)
     energy = numer / denom
 
     def finish(p):
@@ -382,39 +417,52 @@
         jnp.ones((8, LANES), F32), rows_buf[...], (((1,), (1,)), ((), ())),
         precision=HIGH, preferred_element_type=F32,
     )
-    g_z[z] = flat[:1]
-    for d in sorted(range(1, RING), key=lambda d: abs(d - RING // 2)):
-        send(g_z.at[z], g_z.at[z], (gz_sem.at[0], gz_sem.at[1]), on_ring(d))
-    with jax.named_scope("w_gz"):
-        take(gz_sem.at[1], g_z.at[pl.ds(0, RING - 1)])
-    mine = y * STATES + s
-    g_xy[mine] = jnp.sum(g_z[...], axis=0)
-    for d in sorted(range(1, STATES * columns), key=lambda d: abs(d // STATES - 2) + abs(d % STATES - 4) / 2):
-        send(g_xy.at[mine], g_xy.at[mine], (gx_sem.at[0], gx_sem.at[1]), on_face(d))
+    mine = core * RING + z
+    g_z[mine] = flat[:1]
+    rows_out = (gz_sem.at[0], gz_sem.at[1])
+    for d in far_first:
+        send(g_z.at[mine], g_z.at[mine], rows_out, (on_ring(d)[0], chip_states[1]))
+    pl.when(core == 0)(lambda: send(g_z.at[mine], g_z.at[mine], rows_out, partner))
+
+    @pl.when(hub)
+    def _():
+        take(gz_sem.at[1], g_z.at[pl.ds(0, 2 * RING - 1)])
+        place = y * CHIPS + x
+        g_xy[place] = jnp.sum(g_z[...], axis=0)
+        for d in sorted(range(1, STATES * columns), key=lambda d: abs(d // STATES - 2) + abs(d % STATES - 4) / 2):
+            send(g_xy.at[place], g_xy.at[place], (gx_sem.at[0], gx_sem.at[1]), on_face(d))
+
     with jax.named_scope("w_sends"):
         take(halo_send, o_buf.at[pl.ds(0, 6)])
         take(f1_sem.at[0], f1_buf.at[pl.ds(0, 4)])
         take(f2_sem.at[0], f2_in)
         take(f3_sem.at[0], f3_in.at[pl.ds(0, 2 * REACH)])
-        take(ey_sem.at[0], e_y.at[pl.ds(0, columns - 1)])
-        take(ez_sem.at[0], e_z.at[pl.ds(0, RING - 1)])
         take(x_sem.at[0], mixed.at[pl.ds(0, STATES - 1)])
+
+    @pl.when(core == 0)
+    def _():
+        take(ey_sem.at[0], g_z.at[pl.ds(0, columns)])
+        take(gz_sem.at[0], g_z.at[pl.ds(0, RING)])
+        take(gx_sem.at[1], g_xy)
+
+    @pl.when(hub)
+    def _():
+        take(ey_sem.at[0], g_z.at[pl.ds(0, columns - 1)])
+        take(ez_sem.at[0], g_z.at[pl.ds(0, 2 * RING - 1)])
         take(gz_sem.at[0], g_z.at[pl.ds(0, RING - 1)])
-    with jax.named_scope("w_gxy"):
-        take(gx_sem.at[1], g_xy.at[pl.ds(0, STATES * columns - 1)])
+        take(gx_sem.at[1], g_xy.at[pl.ds(0, CHIPS * columns - 1)])
+
     total = jnp.sum(g_xy[...], axis=0)
     picked = jnp.zeros((1, STATES), F32)
     for t in range(STATES):
         picked += jnp.where(s == t, total[:, STATES * t : STATES * t + STATES], 0.0)
     gram_ref[...] = picked / F32(PLANES * ROWS * LANES * slabs)
-    with jax.named_scope("w_last"):
-        take(gx_sem.at[0], g_xy.at[pl.ds(0, STATES * columns - 1)])
+    pl.when(hub)(lambda: take(gx_sem.at[0], g_z.at[pl.ds(0, STATES * columns - 1)]))
 
 
 def solution(mesh):
     slabs = mesh.shape["grid"]
     columns = slabs // RING
-    faces = STATES * columns
     dma = pltpu.SemaphoreType.DMA
 
     def vmem(*shape, dtype=F32):
@@ -467,17 +515,17 @@
                 vmem(6, ROWS, LANES),
                 vmem(PLANES, ROWS, LANES),
                 vmem(PLANES, ROWS, LANES),
-                vmem(columns, 1, LANES),
+                vmem(2 * columns, 1, LANES),
                 vmem(RING, 1, LANES),
                 vmem(PLANES, ROWS, LANES, dtype=jnp.bfloat16),
                 vmem(STATES, ROWS, LANES, dtype=jnp.bfloat16),
                 vmem(LANES, LANES),
-                vmem(RING, 1, LANES),
-                vmem(faces, 1, LANES),
+                vmem(2 * RING, 1, LANES),
+                vmem(CHIPS * columns, 1, LANES),
                 vmem(LANES, 2 * LANES),
                 dma((2,)), dma(()), dma((3,)), dma((2,)), dma((2,)), dma((2,)),
                 dma((2,)), dma((2,)), dma((2,)), dma((2,)), dma((2,)),
-                pltpu.SemaphoreType.REGULAR((3,)),
+                pltpu.SemaphoreType.REGULAR((5,)),
             ],
             compiler_params=pltpu.CompilerParams(
                 collective_id=0, has_side_effects=True, vmem_limit_bytes=32 * 1024 * 1024

time: 45.8 us -> 44.5 us (0.972)
  Pallas kernels: 45 us -> 43.7 us
    pallas_call x1, Pallas kernels: 44.3 us -> 43 us  [on_device(): pl.pallas_call(functools.partial(kernel, slabs), out_shape=(jax.ShapeDtyp...]
where the time goes in v5:
time: 44.5 us; the launch traced here: 44.4 us
  Pallas kernels  43.7 us (98%)
  between operations  0.64 us (1%)
    pallas_call x1, Pallas kernels, on_device(): pl.pallas_call(functools.partial(kernel, slabs), out_shape=(jax.ShapeDtyp...  43 us

profile of v5, /device:TPU:1, one launch (start us, length us, event | category | flops | bytes accessed | tf_op | source)
XLA Modules:
  0.0 44.4 jit_solution(9509073254881156902)
XLA Ops:
  0.6 43.0 %shard_map.41 = (f32[1,8,64,128]{3,2,1,0:T(8,128)S(1)}, f32[1,8]{1,0:T(1,128)S(1)}) custom-call(f32[1,8,64,128]{3,2,1,0:T(8,128)} %o_hbm.1, f32[8,64,128]{2,1,0:T(8,128)} %p_hbm.1), custom_call_target="tpu_custom_call" | custom-call | tf_op jit(solution)/shard_map/pallas_call | solution.py:486
  43.6 0.7 %shard_map.42 = (f32[1,8,64,128]{3,2,1,0:T(8,128)}, f32[1,8]{1,0:T(1,128)}) custom-call(f32[1,8,64,128]{3,2,1,0:T(8,128)S(1)} %get-tuple-element.4.values, f32[1,8]{1,0:T(1,128)S(1)} %get-tuple-element.5.gram), custom_call_target="tpu_custom_call" | custom-call | tf_op jit(solution)/shard_map/pallas_call | solution.py:535

commit v6 on v5

--- a/solution.py
+++ b/solution.py
@@ -392,44 +392,52 @@
         out_ref[0, p] = value
         return value.astype(jnp.bfloat16)
 
-    for step, other in others:
-        to = state_at(step, other)
-        rounded[to] = finish(to)
-        send(rounded.at[to], mixed.at[s], (x_sem.at[0], x_sem.at[1]), (g, to))
-    mixed[s] = finish(s)
-    with jax.named_scope("w_mix"):
-        take(x_sem.at[1], mixed.at[pl.ds(0, STATES - 1)])
-
-    pairs = [(i, j) for i in range(STATES) for j in range(i, STATES)]
-    held = {pair: None for pair in pairs}
-    for block in range(ROWS // 16):
-        values = [mixed[i, 16 * block : 16 * block + 16].astype(F32) for i in range(STATES)]
-        for i, j in pairs:
-            product = values[i] * values[j]
-            product = product[:8] + product[8:]
-            held[i, j] = product if held[i, j] is None else held[i, j] + product
-    for i, j in pairs:
-        row = jnp.sum(held[i, j], 0, keepdims=True)
-        rows_buf[8 * i + j : 8 * i + j + 1] = row
-        if i != j:
-            rows_buf[8 * j + i : 8 * j + i + 1] = row
-    flat = lax.dot_general(
-        jnp.ones((8, LANES), F32), rows_buf[...], (((1,), (1,)), ((), ())),
-        precision=HIGH, preferred_element_type=F32,
-    )
-    mine = core * RING + z
-    g_z[mine] = flat[:1]
-    rows_out = (gz_sem.at[0], gz_sem.at[1])
-    for d in far_first:
-        send(g_z.at[mine], g_z.at[mine], rows_out, (on_ring(d)[0], chip_states[1]))
-    pl.when(core == 0)(lambda: send(g_z.at[mine], g_z.at[mine], rows_out, partner))
+    def to_hub(step):
+        chip = (x + step) & (CHIPS - 1)
+        for plane in (0, 1):
+            rounded[2 * chip + plane] = finish(2 * chip + plane)
+        send(
+            rounded.at[pl.ds(2 * chip, 2)], mixed.at[s], (x_sem.at[0], x_sem.at[1]), (g, 2 * chip + 1)
+        )
+
+    for step in (2, 1, -1):
+        to_hub(step)
+
+    @pl.when(core == 0)
+    def _():
+        to_hub(0)
 
     @pl.when(hub)
     def _():
-        take(gz_sem.at[1], g_z.at[pl.ds(0, 2 * RING - 1)])
+        for plane in (0, 1):
+            mixed[s, plane] = finish(2 * x + plane)
+        take(x_sem.at[1], mixed.at[pl.ds(0, STATES - 1)])
+        pairs = [(i, j) for i in range(STATES) for j in range(i, STATES)]
+        held = {pair: None for pair in pairs}
+        for at in range(2 * ROWS // 16):
+            rows = slice(16 * at % ROWS, 16 * at % ROWS + 16)
+            values = [mixed[i, 16 * at // ROWS, rows].astype(F32) for i in range(STATES)]
+            for i, j in pairs:
+                product = values[i] * values[j]
+                product = product[:8] + product[8:]
+                held[i, j] = product if held[i, j] is None else held[i, j] + product
+        for i, j in pairs:
+            row = jnp.sum(held[i, j], 0, keepdims=True)
+            rows_buf[8 * i + j : 8 * i + j + 1] = row
+            if i != j:
+                rows_buf[8 * j + i : 8 * j + i + 1] = row
+        flat = lax.dot_general(
+            jnp.ones((8, LANES), F32), rows_buf[...], (((1,), (1,)), ((), ())),
+            precision=HIGH, preferred_element_type=F32,
+        )
+        g_z[z] = flat[:1]
+        for d in far_first:
+            send(g_z.at[z], g_z.at[z], (gz_sem.at[0], gz_sem.at[1]), on_ring(d))
+        take(gz_sem.at[1], g_z.at[pl.ds(0, RING - 1)])
         place = y * CHIPS + x
-        g_xy[place] = jnp.sum(g_z[...], axis=0)
-        for d in sorted(range(1, STATES * columns), key=lambda d: abs(d // STATES - 2) + abs(d % STATES - 4) / 2):
+        g_xy[place] = jnp.sum(g_z[:RING], axis=0)
+        order = {d: abs(d // STATES - 2) + abs(d % STATES - 4) / 2 - d % 2 for d in range(1, STATES * columns)}
+        for d in sorted(order, key=order.get):
             send(g_xy.at[place], g_xy.at[place], (gx_sem.at[0], gx_sem.at[1]), on_face(d))
 
     with jax.named_scope("w_sends"):
@@ -437,18 +445,18 @@
         take(f1_sem.at[0], f1_buf.at[pl.ds(0, 4)])
         take(f2_sem.at[0], f2_in)
         take(f3_sem.at[0], f3_in.at[pl.ds(0, 2 * REACH)])
-        take(x_sem.at[0], mixed.at[pl.ds(0, STATES - 1)])
 
     @pl.when(core == 0)
     def _():
         take(ey_sem.at[0], g_z.at[pl.ds(0, columns)])
-        take(gz_sem.at[0], g_z.at[pl.ds(0, RING)])
+        take(x_sem.at[0], mixed.at[pl.ds(0, CHIPS)])
         take(gx_sem.at[1], g_xy)
 
     @pl.when(hub)
     def _():
         take(ey_sem.at[0], g_z.at[pl.ds(0, columns - 1)])
         take(ez_sem.at[0], g_z.at[pl.ds(0, 2 * RING - 1)])
+        take(x_sem.at[0], mixed.at[pl.ds(0, CHIPS - 1)])
         take(gz_sem.at[0], g_z.at[pl.ds(0, RING - 1)])
         take(gx_sem.at[1], g_xy.at[pl.ds(0, CHIPS * columns - 1)])
 
@@ -518,7 +526,7 @@
                 vmem(2 * columns, 1, LANES),
                 vmem(RING, 1, LANES),
                 vmem(PLANES, ROWS, LANES, dtype=jnp.bfloat16),
-                vmem(STATES, ROWS, LANES, dtype=jnp.bfloat16),
+                vmem(STATES, 2, ROWS, LANES, dtype=jnp.bfloat16),
                 vmem(LANES, LANES),
                 vmem(2 * RING, 1, LANES),
                 vmem(CHIPS * columns, 1, LANES),

time: 44.5 us -> 43.8 us (0.984)
  Pallas kernels: 43.7 us -> 43 us
    pallas_call x1, Pallas kernels: 43 us -> 42.3 us  [on_device(): pl.pallas_call(functools.partial(kernel, slabs), out_shape=(jax.ShapeDtyp...]
where the time goes in v6:
time: 43.8 us; the launch traced here: 43.6 us
  Pallas kernels  43 us (98%)
  between operations  0.64 us (1%)
    pallas_call x1, Pallas kernels, on_device(): pl.pallas_call(functools.partial(kernel, slabs), out_shape=(jax.ShapeDtyp...  42.3 us

profile of v6, /device:TPU:1, one launch (start us, length us, event | category | flops | bytes accessed | tf_op | source)
XLA Modules:
  0.0 43.6 jit_solution(16448344909702780563)
XLA Ops:
  0.6 42.3 %shard_map.41 = (f32[1,8,64,128]{3,2,1,0:T(8,128)S(1)}, f32[1,8]{1,0:T(1,128)S(1)}) custom-call(f32[1,8,64,128]{3,2,1,0:T(8,128)} %o_hbm.1, f32[8,64,128]{2,1,0:T(8,128)} %p_hbm.1), custom_call_target="tpu_custom_call" | custom-call | tf_op jit(solution)/shard_map/pallas_call | solution.py:494
  42.9 0.7 %shard_map.42 = (f32[1,8,64,128]{3,2,1,0:T(8,128)}, f32[1,8]{1,0:T(1,128)}) custom-call(f32[1,8,64,128]{3,2,1,0:T(8,128)S(1)} %get-tuple-element.4.values, f32[1,8]{1,0:T(1,128)S(1)} %get-tuple-element.5.gram), custom_call_target="tpu_custom_call" | custom-call | tf_op jit(solution)/shard_map/pallas_call | solution.py:543

commit v7 on v6

--- a/solution.py
+++ b/solution.py
@@ -146,6 +146,12 @@
     ]
     for load in loads:
         load.start()
+    made = matrices()
+    for index in range(6):
+        mats[index] = made[index]
+    wide[:, :LANES] = made[6]
+    wide[:, LANES:] = made[7]
+    rows_buf[...] = jnp.zeros_like(rows_buf)
     with jax.named_scope("w_load"):
         for load in loads:
             load.wait()
@@ -184,12 +190,6 @@
     sems = (halo_send, halo_recv.at[2])
     send(g_out.at[1], g_in.at[0], sems, right)
     send(g_out.at[0], g_in.at[1], sems, left)
-    made = matrices()
-    for index in range(6):
-        mats[index] = made[index]
-    wide[:, :LANES] = made[6]
-    wide[:, LANES:] = made[7]
-    rows_buf[...] = jnp.zeros_like(rows_buf)
     top, bottom = jnp.sum(top, 0, keepdims=True), jnp.sum(bottom, 0, keepdims=True)
     lane_row = iota((1, LANES), 1)
 

time: 43.8 us -> 43.8 us (level)
  no operation moved by 1% of the time
where the time goes in v7:
time: 43.8 us; the launch traced here: 43.6 us
  Pallas kernels  43 us (98%)
  between operations  0.64 us (1%)
    pallas_call x1, Pallas kernels, on_device(): pl.pallas_call(functools.partial(kernel, slabs), out_shape=(jax.ShapeDtyp...  42.3 us

profile of v7, /device:TPU:1, one launch (start us, length us, event | category | flops | bytes accessed | tf_op | source)
XLA Modules:
  0.0 43.6 jit_solution(8868034019768106792)
XLA Ops:
  0.6 42.3 %shard_map.41 = (f32[1,8,64,128]{3,2,1,0:T(8,128)S(1)}, f32[1,8]{1,0:T(1,128)S(1)}) custom-call(f32[1,8,64,128]{3,2,1,0:T(8,128)} %o_hbm.1, f32[8,64,128]{2,1,0:T(8,128)} %p_hbm.1), custom_call_target="tpu_custom_call" | custom-call | tf_op jit(solution)/shard_map/pallas_call | solution.py:494
  42.9 0.7 %shard_map.42 = (f32[1,8,64,128]{3,2,1,0:T(8,128)}, f32[1,8]{1,0:T(1,128)}) custom-call(f32[1,8,64,128]{3,2,1,0:T(8,128)S(1)} %get-tuple-element.4.values, f32[1,8]{1,0:T(1,128)S(1)} %get-tuple-element.5.gram), custom_call_target="tpu_custom_call" | custom-call | tf_op jit(solution)/shard_map/pallas_call | solution.py:543

commit v8 on v6

--- a/solution.py
+++ b/solution.py
@@ -309,8 +309,8 @@
             jnp.where(lane_row < 32, first, pltpu.roll(first, 96, 1)),
             jnp.where(lane_row < 96, pltpu.roll(second, 64, 1), pltpu.roll(second, 32, 1)),
         )
-        for d in far_first:
-            for state in chip_states:
+        for state in chip_states:
+            for d in far_first:
                 send(e_z.at[z], e_z.at[z], (ez_sem.at[0], ez_sem.at[1]), (on_ring(d)[0], state))
         send(e_z.at[z], e_z.at[z], (ez_sem.at[0], ez_sem.at[1]), partner)
 

time: 43.8 us -> 43.8 us (level)
  no operation moved by 1% of the time
where the time goes in v8:
time: 43.8 us; the launch traced here: 43.6 us
  Pallas kernels  43 us (98%)
  between operations  0.64 us (1%)
    pallas_call x1, Pallas kernels, on_device(): pl.pallas_call(functools.partial(kernel, slabs), out_shape=(jax.ShapeDtyp...  42.3 us

profile of v8, /device:TPU:1, one launch (start us, length us, event | category | flops | bytes accessed | tf_op | source)
XLA Modules:
  0.0 43.6 jit_solution(8470023520239512737)
XLA Ops:
  0.6 42.3 %shard_map.41 = (f32[1,8,64,128]{3,2,1,0:T(8,128)S(1)}, f32[1,8]{1,0:T(1,128)S(1)}) custom-call(f32[1,8,64,128]{3,2,1,0:T(8,128)} %o_hbm.1, f32[8,64,128]{2,1,0:T(8,128)} %p_hbm.1), custom_call_target="tpu_custom_call" | custom-call | tf_op jit(solution)/shard_map/pallas_call | solution.py:494
  42.9 0.7 %shard_map.42 = (f32[1,8,64,128]{3,2,1,0:T(8,128)}, f32[1,8]{1,0:T(1,128)}) custom-call(f32[1,8,64,128]{3,2,1,0:T(8,128)S(1)} %get-tuple-element.4.values, f32[1,8]{1,0:T(1,128)S(1)} %get-tuple-element.5.gram), custom_call_target="tpu_custom_call" | custom-call | tf_op jit(solution)/shard_map/pallas_call | solution.py:543
